TPU v7x, 32 devices: a whole 2x2x4 slice. The times are simulated.
32 devices in a mesh: dp: 2 (over x), pipe: 4 (over z), expert: 4 (over y, core).
Axes of the slice: x: 2, y: 2, z: 4, core: 2. Of those that a mesh axis runs over, the one named last changes fastest.
Arguments:
- out_grad: bfloat16 [1024, 4096], P(('dp', 'expert'), 'pipe'), may hold values from -6 to 6
- expert_ids: int32 [1024, 2], P(('dp', 'expert')), may hold values from 0 to 3, all different within a row; in each aligned block of 128 rows (0 to 127, 128 to 255, ...) at most 80 rows name the same one
- combine_weights: float32 [1024, 2], P(('dp', 'expert')), may hold values from 0.1 to 1
- down_weight: bfloat16 [4, 7168, 4096], P('expert', 'pipe'), may hold values from -0.0625 to 0.0625
- saved_pre: bfloat16 [4, 2, 640, 7168], P('expert', None, 'dp', 'pipe'), may hold values from -6 to 6
Outputs:
- pre_grad: bfloat16 [4, 2, 640, 7168], P('expert', None, 'dp', 'pipe')
- w_grad: bfloat16 [4, 7168, 4096], P('expert', 'pipe', 'dp')
- prob_grad: float32 [1024, 2], P(('dp', 'expert'))
Inputs may be any that keep to these rules, and one draw needn't show every extreme that they name: `expert_ids`: the 2 ids of a row differ. In each aligned block of 128 rows (the tokens of one device) no expert is named by more than 80 rows, a bound that some block reaches.
All inputs are finite; a program needn't handle non-finite values.
Results may differ from a plain program's by a relative error of at most 0.0064.
Values may be sent and summed in bfloat16 or wider, within the bound.
A program may use at most 128 MiB of HBM per device.

v0:
```python
import jax
import jax.numpy as jnp
from jax import lax
from jax.sharding import PartitionSpec as P


def body(out_grad, expert_ids, combine_weights, down_weight, saved_pre):
    experts = lax.axis_size("expert")
    slot_count = saved_pre.shape[2]
    capacity = slot_count // experts
    labels = jnp.arange(experts, dtype=jnp.int32)
    onehot = (expert_ids[:, :, None] == labels).astype(jnp.int32)
    per_token = jnp.sum(onehot, axis=1, dtype=jnp.int32)
    before = jnp.cumsum(per_token, axis=0, dtype=jnp.int32) - per_token
    position = jnp.sum(onehot * before[:, None, :], axis=2, dtype=jnp.int32)
    slot_index = expert_ids * capacity + position
    targets = jnp.arange(slot_count, dtype=jnp.int32)
    chosen = slot_index[:, :, None] == targets
    selector = jnp.any(chosen, axis=1).astype(jnp.bfloat16)
    routed = lax.dot_general(
        selector, out_grad, (((0,), (0,)), ((), ())), preferred_element_type=jnp.float32
    ).astype(jnp.bfloat16)
    rounded = lax.optimization_barrier(combine_weights.astype(jnp.bfloat16))
    slot_weight = jnp.sum(
        jnp.where(chosen, rounded.astype(jnp.float32)[:, :, None], 0.0), axis=(0, 1)
    )
    slot_weight = slot_weight.astype(jnp.bfloat16)
    recv_grad, recv_weight = (
        lax.all_to_all(
            routed.reshape(experts, capacity, -1), "expert", split_axis=0, concat_axis=0, tiled=True
        ),
        lax.all_to_all(
            slot_weight.reshape(experts, capacity),
            "expert",
            split_axis=0,
            concat_axis=0,
            tiled=True,
        ),
    )
    local_grad = recv_grad.reshape(slot_count, -1)
    weight_row = recv_weight.reshape(slot_count).astype(jnp.float32)
    gate_pre = saved_pre[0, 0].astype(jnp.float32)
    up_pre = saved_pre[0, 1].astype(jnp.float32)
    activated = jax.nn.silu(gate_pre)
    hidden = activated * up_pre
    hidden_b = hidden.astype(jnp.bfloat16)
    scaled = (weight_row[:, None] * hidden).astype(jnp.bfloat16)
    projection = down_weight[0]
    segment = lax.all_gather(local_grad, "pipe", axis=1, tiled=True)
    back_grad = lax.dot_general(
        segment, projection, (((1,), (1,)), ((), ())), preferred_element_type=jnp.float32
    )
    partial_out = jnp.dot(hidden_b, projection, preferred_element_type=jnp.float32)
    scores = jnp.sum(segment.astype(jnp.float32) * partial_out, axis=1)
    term_cols = lax.dot_general(
        scaled, segment, (((0,), (0,)), ((), ())), preferred_element_type=jnp.float32
    )
    kept_data = term_cols
    back_grad, scores, kept_data = (back_grad, scores, kept_data)
    hidden_grad = weight_row[:, None] * back_grad
    sigmoid_gate = jax.nn.sigmoid(gate_pre)
    gate_grad = hidden_grad * up_pre * sigmoid_gate * (1.0 + gate_pre * (1.0 - sigmoid_gate))
    up_grad = hidden_grad * activated
    pre_grad = jnp.stack([gate_grad, up_grad]).astype(jnp.bfloat16)[None]
    total_score = lax.psum(scores, "pipe")
    returned = lax.all_to_all(
        total_score.reshape(experts, capacity), "expert", split_axis=0, concat_axis=0, tiled=True
    )
    returned = returned.reshape(slot_count)
    prob_grad = jnp.sum(jnp.where(chosen, returned[None, None, :], 0.0), axis=2)
    w_grad = lax.psum_scatter(kept_data.astype(jnp.bfloat16), "dp", scatter_dimension=1, tiled=True)
    return (pre_grad, w_grad[None], prob_grad)


def solution(mesh):
    in_specs = (
        P(("dp", "expert"), "pipe"),
        P(("dp", "expert"), None),
        P(("dp", "expert"), None),
        P("expert", "pipe", None),
        P("expert", None, "dp", "pipe"),
    )
    out_specs = (
        P("expert", None, "dp", "pipe"),
        P("expert", "pipe", "dp"),
        P(("dp", "expert"), None),
    )
    return jax.shard_map(body, mesh=mesh, in_specs=in_specs, out_specs=out_specs, check_vma=False)
```

profile of v0, /device:TPU:0, one launch (start us, length us, event | category | flops | bytes accessed | tf_op | source)
XLA Modules:
  0.0 302.3 jit_solution(2849366943560753517)
XLA Ops:
  7.2 0.0 copy-start
  7.2 0.0 all-gather.2.cloned.1.call-start
  7.2 0.7 convert_reduce_fusion
  8.0 0.1 copy.18
  8.1 0.2 reduce_window_sum.11
  8.2 0.1 copy.20
  8.3 0.7 select_reduce_fusion.2
  9.0 0.7 multiply_add_fusion
  9.8 0.0 copy-done
  9.8 0.3 convolution_convert_fusion.1
  10.1 14.4 %all_to_all.20 = bf16[4,80,1024]{2,1,0:T(8,128)(2,1)} all-to-all(bf16[4,80,1024]{2,1,0:T(8,128)(2,1)S(1)} %bitcast.76), channel_id=1, replica_groups=mesh['dp'=2,'pipe'=4,'expert'=4] {'expert'}, dimensions={0} | all-to-all | bytes 1310720 | tf_op jit(solution)/shard_map/all_to_all | solution.py:29
  24.5 0.0 all-gather.2.cloned.1.call-update
  24.5 0.0 copy-start.2
  24.5 55.6 %all-gather.2.cloned.1.call-done = bf16[320,4096]{1,0:T(8,128)(2,1)} async-done(((bf16[320,1024]{1,0:T(8,128)(2,1)}), bf16[320,4096]{1,0:T(8,128)(2,1)}) %all-gather.2.cloned.1.call-update) | async-done | bytes 2621456 | tf_op jit(solution)/shard_map/all_gather | solution.py:49
  80.1 12.0 %fusion.28 = f32[320]{0:T(512)S(1)} fusion(bf16[1,1792,4096]{2,1,0:T(8,128)(2,1)} %param.8, bf16[320,4096]{1,0:T(8,128)(2,1)} %all-gather.2.cloned.1.call-done, bf16[1,2,320,1792]{3,2,1,0:T(8,128)(2,1)} %param.9), kind=kOutput, calls=%fused_computation.32 | convolution fusion | flops 4706139648 | bytes 19596544 | tf_op jit(solution)/shard_map/dot_general | solution.py:53
  92.1 0.1 all_to_all.15
  92.2 9.8 %psum.7 = f32[4,1,80]{2,1,0:T(1,128)} all-reduce(f32[4,1,80]{2,1,0:T(1,128)S(1)} %all_to_all.15), channel_id=1, replica_groups=mesh['dp'=2,'pipe'=4,'expert'=4] {'pipe'}, use_global_device_ids=true, to_apply=%region_7.8 | all-reduce | flops 320 | bytes 2560 | tf_op jit(solution)/shard_map/psum | solution.py:65
  102.0 3.2 %all-to-all-start.2 = ((f32[4,1,80]{2,1,0:T(1,128)}), f32[4,1,80]{2,1,0:T(1,128)S(1)}, u32[]{:S(2)}, u32[]{:S(2)}) async-start(f32[4,1,80]{2,1,0:T(1,128)} %psum.7), calls=%async_computation.3 | async-start | bytes 4096 | tf_op jit(solution)/shard_map/all_to_all | solution.py:66
  105.2 0.0 reduce-scatter.2.cloned.1.call-start
  105.3 3.6 %all-to-all-done.2 = f32[4,1,80]{2,1,0:T(1,128)S(1)} async-done(((f32[4,1,80]{2,1,0:T(1,128)}), f32[4,1,80]{2,1,0:T(1,128)S(1)}, u32[]{:S(2)}, u32[]{:S(2)}) %all-to-all-start.2) | async-done | bytes 1312 | tf_op jit(solution)/shard_map/all_to_all | solution.py:66
  108.9 0.5 broadcast.38
  109.4 0.7 reduce.7
  110.0 0.1 broadcast_in_dim.39
  110.1 0.7 select_reduce_fusion
  110.8 0.1 convert_element_type.100
  110.9 6.1 %all_to_all.21 = bf16[4,1,80]{2,1,0:T(2,128)(2,1)S(1)} all-to-all(bf16[4,1,80]{2,1,0:T(2,128)(2,1)S(1)} %convert_element_type.100), channel_id=1, replica_groups=mesh['dp'=2,'pipe'=4,'expert'=4] {'expert'}, dimensions={0} | all-to-all | bytes 1280 | tf_op jit(solution)/shard_map/all_to_all | solution.py:32
  117.0 0.1 reshape.94
  117.1 13.3 %convolution_convert_fusion = bf16[1792,4096]{1,0:T(8,128)(2,1)} fusion(bf16[320,4096]{1,0:T(8,128)(2,1)S(1)} %copy-done.1, f32[320]{0:T(512)S(1)} %reshape.94, bf16[1,2,320,1792]{3,2,1,0:T(8,128)(2,1)} %param.9), kind=kOutput, calls=%fused_computation | convolution fusion | flops 4710121472 | bytes 19596544 | tf_op jit(solution)/shard_map/dot_general | solution.py:55
  130.4 0.0 reduce-scatter.2.cloned.1.call-update
  130.4 13.5 %fusion.36 = (bf16[1,1,320,1792]{3,2,1,0:T(8,128)(2,1)S(1)}, bf16[1,1,320,1792]{3,2,1,0:T(8,128)(2,1)S(1)}) fusion(bf16[1,2,320,1792]{3,2,1,0:T(8,128)(2,1)} %param.9, bf16[320,4096]{1,0:T(8,128)(2,1)} %all-gather.2.cloned.1.call-done, bf16[1,1792,4096]{2,1,0:T(8,128)(2,1)} %param.8, f32[320]{0:T(512)S(1)} %reshape.94), kind=kOutput, calls=%fused_computation.37 | convolution fusion | flops 4706795520 | bytes 21890304 | tf_op jit(solution)/shard_map/dot_general | solution.py:50
  143.9 1.6 pad_maximum_fusion
  145.4 150.0 %reduce-scatter.2.cloned.1.call-done = bf16[1792,2048]{1,0:T(8,128)(2,1)} async-done(((bf16[1792,4096]{1,0:T(8,128)(2,1)}), bf16[1792,2048]{1,0:T(8,128)(2,1)}) %reduce-scatter.2.cloned.1.call-update) | async-done | bytes 7340048 | tf_op jit(solution)/shard_map/reduce_scatter | solution.py:71
  (8 shorter events, 0.1 us)
Async XLA Ops:
  7.2 2.6 copy-start
  7.2 73.0 %all-gather.2.cloned.1.call-start = ((), (), s32[]{:S(2)}) async-start(), calls=%async_computation.4 | async-start | bytes 3276800 | tf_op jit(solution)/shard_map/all_gather | solution.py:49
  24.5 80.8 %copy-start.2 = (f32[128,2]{0,1:T(2,128)S(1)}, f32[128,2]{0,1:T(2,128)}, u32[]{:S(2)}) copy-start(f32[128,2]{0,1:T(2,128)} %param.7) | copy-start | bytes 3076
  80.1 37.0 %copy-start.1 = (bf16[320,4096]{1,0:T(8,128)(2,1)S(1)}, bf16[320,4096]{1,0:T(8,128)(2,1)}, u32[]{:S(2)}) copy-start(bf16[320,4096]{1,0:T(8,128)(2,1)} %all-gather.2.cloned.1.call-done) | copy-start | bytes 7864324
  102.0 6.9 %all-to-all-start.2 = ((f32[4,1,80]{2,1,0:T(1,128)}), f32[4,1,80]{2,1,0:T(1,128)S(1)}, u32[]{:S(2)}, u32[]{:S(2)}) async-start(f32[4,1,80]{2,1,0:T(1,128)} %psum.7), calls=%async_computation.3 | async-start | bytes 4096 | tf_op jit(solution)/shard_map/all_to_all | solution.py:66
  105.2 190.2 %reduce-scatter.2.cloned.1.call-start = ((), (), s32[]{:S(2)}) async-start(), calls=%async_computation.5 | async-start | bytes 22020096 | tf_op jit(solution)/shard_map/reduce_scatter | solution.py:71
Sparse Core Ops, SparseCore 0:
  24.6 55.4 all-gather.1
  130.5 164.8 reduce-scatter.1
where the time goes:
time: 303 us; the launch traced here: 302 us
  waiting for transfers between devices  209 us (69%)
  matrix products  39 us (13%)
  blocking collectives  30.3 us (10%)
  between operations  14.1 us (5%)
  other arithmetic  5.33 us (2%)
  starting transfers between devices  3.3 us (1%)
    reduce_scatter x1, waiting for transfers between devices, body(): lax.psum_scatter(kept_data.astype(jnp.bfloat16), 'dp', scatter_dimension=...  150 us
    all_gather x1, waiting for transfers between devices, body(): segment = lax.all_gather(local_grad, 'pipe', axis=1, tiled=True)  55.6 us
    all_to_all x1, blocking collectives, body(): lax.all_to_all(routed.reshape(experts, capacity, -1), 'expert', split_axi...  14.4 us
    dot_general x1, matrix products, body(): lax.dot_general(segment, projection, (((1,), (1,)), ((), ())), preferred_...  13.5 us
    dot_general x1, matrix products, body(): lax.dot_general(scaled, segment, (((0,), (0,)), ((), ())), preferred_elem...  13.3 us
    dot_general x1, matrix products, body(): jnp.dot(hidden_b, projection, preferred_element_type=jnp.float32)  12 us
    psum x1, blocking collectives, body(): total_score = lax.psum(scores, 'pipe')  9.79 us
    all_to_all x1, blocking collectives, body(): lax.all_to_all(slot_weight.reshape(experts, capacity), 'expert', split_ax...  6.08 us
  transfers between devices with their start and end apart: 3, of which 3 were waited for; matrix products, arithmetic and copies ran while one was open for 5% of the time, Pallas kernels for 0%

commit v1 on v0

v1 whole, which is shorter than its diff:
```python
import functools
import jax
import jax.numpy as jnp
from jax import lax
from jax.experimental import pallas as pl
from jax.experimental.pallas import tpu as pltpu
from jax.sharding import PartitionSpec as P

MESH = pl.DeviceIdType.MESH


def gather_kernel(dims, own_ref, meta_ref, raw_ref, oth_ref, metas_ref,
                  zs, zr, es, er, xs, xr, ms, mr, loc):
    dp, n, experts, cpd = dims
    d, p, e = lax.axis_index("dp"), lax.axis_index("pipe"), lax.axis_index("expert")
    group = dp * experts
    me = d * experts + e
    has_up, has_down = p < n - 1, p > 0
    masks = []
    m = experts // 2
    while m:
        masks.append(m)
        m //= 2

    def flip(value, mask):
        return value + mask * (1 - 2 * (lax.rem(value // mask, 2)))

    def peer(k):
        t = lax.rem(me + k, group)
        return {"dp": t // experts, "pipe": p, "expert": lax.rem(t, experts)}

    def source(k):
        return lax.rem(me + group - k, group)

    barrier = pltpu.get_barrier_semaphore()

    def greet(k, c):
        pl.semaphore_signal(barrier, inc=1, device_id=peer(k), device_id_type=MESH)
        return c

    lax.fori_loop(1, group, greet, 0)

    @pl.when(has_up)
    def _():
        pl.semaphore_signal(barrier, inc=1, device_id={"dp": d, "pipe": p + 1, "expert": e}, device_id_type=MESH)

    @pl.when(has_down)
    def _():
        pl.semaphore_signal(barrier, inc=1, device_id={"dp": d, "pipe": p - 1, "expert": e}, device_id_type=MESH)

    pl.semaphore_wait(barrier, group - 1 + has_up.astype(jnp.int32) + has_down.astype(jnp.int32))

    def meta_copy(k, slot):
        return pltpu.make_async_remote_copy(
            src_ref=meta_ref, dst_ref=metas_ref.at[slot], send_sem=ms.at[k], recv_sem=mr.at[k],
            device_id=peer(k), device_id_type=MESH)

    def z_copy(src, q, s, where):
        return pltpu.make_async_remote_copy(
            src_ref=src, dst_ref=raw_ref.at[q, e], send_sem=zs.at[where, s], recv_sem=zr.at[where, s],
            device_id={"dp": d, "pipe": p + (1 if where == 0 else -1), "expert": e}, device_id_type=MESH)

    def unit_view(unit, b):
        kind, i = unit
        if kind == "own":
            return raw_ref.at[i, b]
        return oth_ref.at[kind, i, b]

    def unit_sem(unit):
        kind, i = unit
        return i if kind == "own" else n + kind * cpd + i

    def e_copy(unit, phase, i, src=None):
        block = e
        for j in range(phase):
            if (i // (1 << j)) % 2:
                block = flip(block, masks[j])
        k = (1 << phase) - 1 + i
        u = unit_sem(unit)
        view = unit_view(unit, block)
        return pltpu.make_async_remote_copy(
            src_ref=view if src is None else src, dst_ref=view, send_sem=es.at[u, k], recv_sem=er.at[u, k],
            device_id={"dp": d, "pipe": p, "expert": flip(e, masks[phase])}, device_id_type=MESH)

    def first(unit, src=None):
        for phase in range(len(masks)):
            e_copy(unit, phase, 0, src).start()

    def rest(unit):
        for phase in range(len(masks)):
            for i in range(1 << phase):
                e_copy(unit, phase, i).wait_recv()
                arrived = i + (1 << phase)
                for later in range(phase + 1, len(masks)):
                    e_copy(unit, later, arrived).start()

    def drain(unit):
        for phase in range(len(masks)):
            for i in range(1 << phase):
                e_copy(unit, phase, i).wait_send()

    def x_copy(k, q, src):
        o = lax.rem(d + k, dp)
        i = q - o * cpd
        return o, pltpu.make_async_remote_copy(
            src_ref=src, dst_ref=oth_ref.at[k - 1, i, e], send_sem=xs.at[k - 1, i], recv_sem=xr.at[k - 1, i],
            device_id={"dp": o, "pipe": p, "expert": e}, device_id_type=MESH)

    def x_send(q, src):
        for k in range(1, dp):
            o = lax.rem(d + k, dp)

            @pl.when(q // cpd == o)
            def _():
                x_copy(k, q, src)[1].start()

    @pl.when(has_up)
    def _():
        z_copy(own_ref, p, 0, 0).start()

    @pl.when(has_down)
    def _():
        z_copy(own_ref, p, 0, 1).start()

    first(("own", p), own_ref)
    x_send(p, own_ref)

    def metas(k, c):
        meta_copy(k, me).start()
        return c

    lax.fori_loop(1, group, metas, 0)
    local = pltpu.make_async_copy(own_ref, raw_ref.at[p, e], loc.at[0])
    local.start()
    local_meta = pltpu.make_async_copy(meta_ref, metas_ref.at[me], loc.at[1])
    local_meta.start()

    for s in range(1, n):
        @pl.when(p - s >= 0)
        def _():
            q = p - s
            z_copy(raw_ref.at[q, e], q, s - 1, 0).wait_recv()

            @pl.when(has_up)
            def _():
                z_copy(raw_ref.at[q, e], q, s, 0).start()

            first(("own", q))
            x_send(q, raw_ref.at[q, e])

        @pl.when(p + s < n)
        def _():
            q = p + s
            z_copy(raw_ref.at[q, e], q, s - 1, 1).wait_recv()

            @pl.when(has_down)
            def _():
                z_copy(raw_ref.at[q, e], q, s, 1).start()

            first(("own", q))
            x_send(q, raw_ref.at[q, e])

    rest(("own", p))
    for s in range(1, n):
        @pl.when(p - s >= 0)
        def _():
            rest(("own", p - s))

        @pl.when(p + s < n)
        def _():
            rest(("own", p + s))

    others = [(k - 1, i) for k in range(1, dp) for i in range(cpd)]
    for kind, i in others:
        pltpu.make_async_remote_copy(
            src_ref=oth_ref.at[kind, i, e], dst_ref=oth_ref.at[kind, i, e], send_sem=xs.at[kind, i],
            recv_sem=xr.at[kind, i], device_id={"dp": lax.rem(d + kind + 1, dp), "pipe": p, "expert": e},
            device_id_type=MESH).wait_recv()
        first((kind, i))
    for unit in others:
        rest(unit)

    for q in range(n):
        drain(("own", q))
    for unit in others:
        drain(unit)
        x_copy(unit[0] + 1, lax.rem(d + unit[0] + 1, dp) * cpd + unit[1], own_ref)[1].wait_send()
    for s in range(n):
        @pl.when((p - s >= 0) & has_up)
        def _():
            z_copy(own_ref, p - s, s, 0).wait_send()

        @pl.when((p + s < n) & has_down)
        def _():
            z_copy(own_ref, p + s, s, 1).wait_send()

    def metas_done(k, c):
        meta_copy(k, me).wait_send()
        meta_copy(k, source(k)).wait_recv()
        return c

    lax.fori_loop(1, group, metas_done, 0)
    local.wait()
    local_meta.wait()


def gather(own, meta, dp, n, experts):
    tokens, cw = own.shape
    cpd = n // dp
    group = dp * experts
    vm = pl.BlockSpec(memory_space=pltpu.VMEM)
    units = n + (dp - 1) * cpd
    dma = pltpu.SemaphoreType.DMA
    return pl.pallas_call(
        functools.partial(gather_kernel, (dp, n, experts, cpd)),
        out_shape=(
            jax.ShapeDtypeStruct((n, experts, tokens, cw), own.dtype),
            jax.ShapeDtypeStruct((dp - 1, cpd, experts, tokens, cw), own.dtype),
            jax.ShapeDtypeStruct((group,) + meta.shape, meta.dtype),
        ),
        in_specs=[vm, vm],
        out_specs=(vm, vm, vm),
        scratch_shapes=[
            dma((2, n)), dma((2, n)),
            dma((units, experts - 1)), dma((units, experts - 1)),
            dma((dp - 1, cpd)), dma((dp - 1, cpd)),
            dma((group,)), dma((group,)), dma((2,)),
        ],
        compiler_params=pltpu.CompilerParams(
            collective_id=0, has_side_effects=True, vmem_limit_bytes=48 * 1024 * 1024),
        cost_estimate=pl.CostEstimate(flops=40_000_000_000, bytes_accessed=60_000_000, transcendentals=0),
    )(own, meta)


def body(out_grad, expert_ids, combine_weights, down_weight, saved_pre):
    experts, dp, n = lax.axis_size("expert"), lax.axis_size("dp"), lax.axis_size("pipe")
    e, d = lax.axis_index("expert"), lax.axis_index("dp")
    slot_count = saved_pre.shape[2]
    capacity = slot_count // experts
    tokens = out_grad.shape[0]

    gate_pre = saved_pre[0, 0].astype(jnp.float32)
    up_pre = saved_pre[0, 1].astype(jnp.float32)
    sigmoid_gate = jax.nn.sigmoid(gate_pre)
    activated = gate_pre * sigmoid_gate
    hidden_b = (activated * up_pre).astype(jnp.bfloat16)
    hidden_all = [hidden_b]
    for k in range(1, dp):
        hidden_all.append(lax.ppermute(hidden_b, "dp", [(i, (i + k) % dp) for i in range(dp)]))

    labels = jnp.arange(experts, dtype=jnp.int32)
    hit = expert_ids.T[None, :, :] == labels[:, None, None]
    named = jnp.any(hit, axis=1)
    earlier = jnp.arange(tokens)[:, None] < jnp.arange(tokens)[None, :]
    position = jnp.dot(named.astype(jnp.bfloat16), earlier.astype(jnp.bfloat16),
                       preferred_element_type=jnp.float32)
    position = jnp.where(named, position, -1.0)
    rounded = lax.optimization_barrier(combine_weights.astype(jnp.bfloat16)).astype(jnp.float32)
    weight = jnp.sum(jnp.where(hit, rounded.T[None], 0.0), axis=1)
    meta = jnp.concatenate([position, weight], axis=0)

    raw, oth, metas = gather(out_grad, meta, dp, n, experts)

    metas = metas.reshape(dp, experts, 2 * experts, tokens)
    where_all = lax.dynamic_index_in_dim(metas, e, 2, keepdims=False)
    weight_all = lax.dynamic_index_in_dim(metas, experts + e, 2, keepdims=False)
    slots = jnp.arange(capacity, dtype=jnp.float32)

    def pick(k):
        at = lax.rem(d - k + dp, dp)
        where = lax.dynamic_index_in_dim(where_all, at, 0, keepdims=False)
        wt = lax.dynamic_index_in_dim(weight_all, at, 0, keepdims=False)
        chosen = where[:, None, :] == slots[None, :, None]
        return chosen, jnp.where(chosen, wt[:, None, :], 0.0)

    def route(sel, data):
        out = lax.dot_general(sel.astype(jnp.bfloat16), data, (((2,), (2,)), ((0,), (1,))),
                              preferred_element_type=jnp.float32)
        return out.astype(jnp.bfloat16).reshape(slot_count, -1)

    chosen, weighted = pick(0)
    weight_row = jnp.sum(weighted, axis=2).reshape(slot_count)
    segment = route(chosen, raw)
    cpd = n // dp
    mine = lax.dynamic_slice_in_dim(raw, d * cpd, cpd, 0)
    segs = [route(weighted, mine)]
    for k in range(1, dp):
        segs.append(route(pick(k)[1], oth[k - 1]))

    back_grad = lax.dot_general(segment, down_weight[0], (((1,), (1,)), ((), ())),
                                preferred_element_type=jnp.float32)
    scores = jnp.sum(hidden_b.astype(jnp.float32) * back_grad, axis=1)
    hidden_grad = weight_row[:, None] * back_grad
    gate_grad = hidden_grad * up_pre * sigmoid_gate * (1.0 + gate_pre * (1.0 - sigmoid_gate))
    up_grad = hidden_grad * activated
    pre_grad = jnp.stack([gate_grad, up_grad]).astype(jnp.bfloat16)[None]

    total = scores.reshape(experts, capacity)
    part = total
    for k in range(1, n):
        total = total + lax.ppermute(part, "pipe", [(i, (i + k) % n) for i in range(n)])
    returned = lax.dynamic_update_slice_in_dim(
        jnp.zeros_like(total), lax.dynamic_slice_in_dim(total, e, 1, 0), e, 0)
    for k in range(1, experts):
        block = lax.dynamic_slice_in_dim(total, lax.rem(e + k, experts), 1, 0)
        got = lax.ppermute(block, "expert", [(i, (i + k) % experts) for i in range(experts)])
        returned = lax.dynamic_update_slice_in_dim(returned, got, lax.rem(e - k + experts, experts), 0)
    place = position[:, :, None] == slots[None, None, :]
    by_expert = jnp.sum(jnp.where(place, returned[:, None, :], 0.0), axis=2)
    prob_grad = jnp.sum(jnp.where(hit, by_expert[:, None, :], 0.0), axis=0).T

    w_grad = lax.dot_general(
        jnp.concatenate(hidden_all, axis=0), jnp.concatenate(segs, axis=0),
        (((0,), (0,)), ((), ())), preferred_element_type=jnp.float32).astype(jnp.bfloat16)
    return (pre_grad, w_grad[None], prob_grad)


def solution(mesh):
    in_specs = (
        P(("dp", "expert"), "pipe"),
        P(("dp", "expert"), None),
        P(("dp", "expert"), None),
        P("expert", "pipe", None),
        P("expert", None, "dp", "pipe"),
    )
    out_specs = (
        P("expert", None, "dp", "pipe"),
        P("expert", "pipe", "dp"),
        P(("dp", "expert"), None),
    )
    return jax.shard_map(body, mesh=mesh, in_specs=in_specs, out_specs=out_specs, check_vma=False)
```

time: 303 us -> 115 us (0.38)
  waiting for transfers between devices: 209 us -> 13.1 us
  Pallas kernels: 0 us -> 50.1 us
  blocking collectives: 30.3 us -> 0 us
  between operations: 14.1 us -> 0.82 us
  local copies, waits for them, and re-layouts: 1.05 us -> 10.7 us
  matrix products: 39 us -> 30.3 us
    reduce_scatter x1 -> x0, waiting for transfers between devices: 150 us -> none  [body(): lax.psum_scatter(kept_data.astype(jnp.bfloat16), 'dp', scatter_dimension=...]
    all_gather x1 -> x0, waiting for transfers between devices: 55.6 us -> none  [body(): segment = lax.all_gather(local_grad, 'pipe', axis=1, tiled=True)]
    pallas_call x0 -> x1, Pallas kernels: none -> 50.1 us  [gather(): pl.pallas_call(functools.partial(gather_kernel, (dp, n, experts, cpd)), o...]
    all_to_all x2 -> x0, blocking collectives: 20.5 us -> none  [the longest x1 14.4 us: body(): lax.all_to_all(routed.reshape(experts, capacity, -1), 'expert', split_axi...]
    ppermute x0 -> x7, waiting for transfers between devices: none -> 13.1 us  [the longest x1 10.2 us: body(): lax.ppermute(hidden_b, 'dp', [(i, (i + k) % dp) for i in range(dp)])]
    psum x1 -> x0, blocking collectives: 9.79 us -> none  [body(): total_score = lax.psum(scores, 'pipe')]
    dot_general x4 -> x6, matrix products: 39 us -> 30.3 us  [the longest x1 13.9 us: body(): lax.dot_general(segment, down_weight[0], (((1,), (1,)), ((), ())), prefer...]
    convert_element_type x2 -> x3, local copies, waits for them, and re-layouts: 0.17 us -> 6.04 us  [route(): return out.astype(jnp.bfloat16).reshape(slot_count, -1)]
  transfers between devices with their start and end apart: 3 -> 7, of which waited for: 3 -> 3; matrix products, arithmetic and copies ran while one was open for 5% -> 11% of each run, Pallas kernels for 0% -> 0%
where the time goes in v1:
time: 115 us; the launch traced here: 114 us
  Pallas kernels  50.1 us (44%)
  matrix products  30.3 us (26%)
  waiting for transfers between devices  13.1 us (11%)
  local copies, waits for them, and re-layouts  10.7 us (9%)
  other arithmetic  5.79 us (5%)
  starting transfers between devices  3.78 us (3%)
    pallas_call x1, Pallas kernels, gather(): pl.pallas_call(functools.partial(gather_kernel, (dp, n, experts, cpd)), o...  50.1 us
    dot_general x1, matrix products, body(): lax.dot_general(segment, down_weight[0], (((1,), (1,)), ((), ())), prefer...  13.9 us
    ppermute x1, waiting for transfers between devices, body(): lax.ppermute(hidden_b, 'dp', [(i, (i + k) % dp) for i in range(dp)])  10.2 us
    dot_general x1, matrix products, body(): lax.dot_general(jnp.concatenate(hidden_all, axis=0), jnp.concatenate(segs...  9.57 us
    dot_general x3, matrix products, route(): lax.dot_general(sel.astype(jnp.bfloat16), data, (((2,), (2,)), ((0,), (1,...  6.67 us
    convert_element_type x3, local copies, waits for them, and re-layouts, route(): return out.astype(jnp.bfloat16).reshape(slot_count, -1)  6.04 us
    unnamed x7, local copies, waits for them, and re-layouts  4.29 us
    ppermute x3, waiting for transfers between devices, body(): lax.ppermute(block, 'expert', [(i, (i + k) % experts) for i in range(expe...  2.86 us
  transfers between devices with their start and end apart: 7, of which 3 were waited for; matrix products, arithmetic and copies ran while one was open for 11% of the time, Pallas kernels for 0%

profile of v1, /device:TPU:0, one launch (start us, length us, event | category | flops | bytes accessed | tf_op | source)
XLA Modules:
  0.0 114.5 jit_solution(11245379757416998777)
XLA Ops:
  0.7 0.7 fusion.47
  1.4 0.7 convert_element_type.51
  2.0 0.7 select_reduce_fusion.3
  2.7 0.1 convolution_select_fusion
  2.9 0.9 copy-done
  3.8 50.1 %shard_map.76 = (bf16[4,4,128,1024]{3,2,1,0:T(8,128)(2,1)}, bf16[1,2,4,128,1024]{4,3,2,1,0:T(8,128)(2,1)S(1)}, f32[8,8,128]{2,1,0:T(8,128)S(1)}) custom-call(bf16[128,1024]{1,0:T(8,128)(2,1)S(1)} %copy-done, f32[8,128]{1,0:T(8,128)S(1)} %pad_maximum_fusion.1.meta_ref), custom_call_target="tpu_custom_call" | custom-call | flops 40000000000 | bytes 60000000 | tf_op jit(solution)/shard_map/pallas_call | solution.py:214
  53.9 0.1 select_reduce_fusion
  54.1 0.1 mul.37
  54.2 3.0 %fusion.23 = bf16[4,80,4,1024]{3,1,2,0:T(8,128)(2,1)S(1)} fusion(bf16[4,4,128,1024]{3,2,1,0:T(8,128)(2,1)} %get-tuple-element.7, f32[4,128]{1,0:T(4,128)S(1)} %bitcast.76), kind=kOutput, calls=%fused_computation.32 | convolution fusion | flops 336896000 | bytes 6817792 | tf_op jit(solution)/shard_map/dot_general | solution.py:277
  57.2 2.0 %copy.18 = bf16[4,80,4,1024]{3,2,1,0:T(4,128)(2,1)S(1)} copy(bf16[4,80,4,1024]{3,1,2,0:T(8,128)(2,1)S(1)} %fusion.23) | data formatting | bytes 5242880 | tf_op jit(solution)/shard_map/convert_element_type | solution.py:279
  59.2 2.6 %copy.26 = bf16[40,8,4,1024]{3,1,2,0:T(8,128)(2,1)} copy(bf16[40,8,4,1024]{3,2,1,0:T(4,128)(2,1)S(1)} %bitcast.69) | data formatting | bytes 5242880
  61.9 13.9 %multiply_reduce_fusion = (f32[320]{0:T(512)S(1)}, bf16[320,1792]{1,0:T(8,128)(2,1)}, bf16[1,1,320,1792]{3,2,1,0:T(8,128)(2,1)S(1)}, bf16[1,1,320,1792]{3,2,1,0:T(8,128)(2,1)}) fusion(bf16[1,2,320,1792]{3,2,1,0:T(8,128)(2,1)} %param.9, f32[320]{0:T(512)S(1)} %mul.37, bf16[320,4096]{1,0:T(8,128)(2,1)} %bitcast.72, bf16[1,1792,4096]{2,1,0:T(8,128)(2,1)} %param.8), kind=kOutput, calls=%fused_computation.26 | convolution fusion | flops 4709662208 | bytes 23038464 | tf_op jit(solution)/shard_map/dot_general | solution.py:290
  75.7 0.1 reshape.103
  75.8 0.5 collective-permute-start.3
  76.4 1.5 %collective-permute-start.1 = (f32[4,80]{1,0:T(4,128)S(1)}, f32[4,80]{1,0:T(4,128)S(1)}, u32[]{:S(2)}, u32[]{:S(2)}) collective-permute-start(f32[4,80]{1,0:T(4,128)S(1)} %reshape.103), channel_id=1, source_target_pairs={{0,4},{4,8},{8,12},{12,0},{1,5},{5,9},{9,13},{13,1},{2,6},{6,10},{... | collective-permute-start | bytes 3848 | tf_op jit(solution)/shard_map/ppermute | solution.py:301
  77.9 0.6 collective-permute-start
  78.4 2.9 %pad_maximum_fusion = bf16[1,2,320,1792]{3,2,1,0:T(8,128)(2,1)} fusion(bf16[1,1,320,1792]{3,2,1,0:T(8,128)(2,1)S(1)} %get-tuple-element.13, bf16[1,1,320,1792]{3,2,1,0:T(8,128)(2,1)} %get-tuple-element.14), kind=kLoop, calls=%fused_computation.22 | loop fusion | flops 1146880 | bytes 4587520 | tf_op jit(solution)/shard_map/stack | solution.py:296
  81.3 2.1 %fusion.26 = bf16[4,80,2,1024]{3,1,2,0:T(8,128)(2,1)S(1)} fusion(f32[4,128]{1,0:T(4,128)S(1)} %bitcast.79, f32[4,128]{1,0:T(4,128)S(1)} %bitcast.77, bf16[4,4,128,1024]{3,2,1,0:T(8,128)(2,1)} %get-tuple-element.7, s32[]{:T(128)S(6)} %select_n.75), kind=kOutput, calls=%fused_computation.33 | convolution fusion | flops 168509440 | bytes 3411972 | tf_op jit(solution)/shard_map/dot_general | solution.py:277
  83.4 1.6 %fusion.29 = bf16[4,80,2,1024]{3,1,2,0:T(8,128)(2,1)} fusion(f32[4,128]{1,0:T(4,128)S(1)} %bitcast.81, f32[4,128]{1,0:T(4,128)S(1)} %bitcast.80, bf16[1,2,4,128,1024]{4,3,2,1,0:T(8,128)(2,1)S(1)} %get-tuple-element.8), kind=kOutput, calls=%fused_computation.34 | convolution fusion | flops 168509440 | bytes 3411968 | tf_op jit(solution)/shard_map/dot_general | solution.py:277
  84.9 2.7 %copy.22 = bf16[4,80,2,1024]{3,2,1,0:T(2,128)(2,1)S(1)} copy(bf16[4,80,2,1024]{3,1,2,0:T(8,128)(2,1)} %fusion.29) | data formatting | bytes 2621440 | tf_op jit(solution)/shard_map/convert_element_type | solution.py:279
  87.6 0.4 copy.28
  88.0 1.4 %copy.20 = bf16[4,80,2,1024]{3,2,1,0:T(2,128)(2,1)S(1)} copy(bf16[4,80,2,1024]{3,1,2,0:T(8,128)(2,1)S(1)} %fusion.26) | data formatting | bytes 2621440 | tf_op jit(solution)/shard_map/convert_element_type | solution.py:279
  89.3 0.4 copy.27
  89.8 0.1 collective-permute-start.6
  89.8 0.5 collective-permute-start.4
  90.3 0.6 collective-permute-start.5
  91.0 1.9 %collective-permute-done.4 = f32[1,80]{1,0:T(1,128)S(1)} collective-permute-done((f32[1,80]{1,0:T(1,128)S(1)}, f32[1,80]{1,0:T(1,128)S(1)}, u32[]{:S(2)}, u32[]{:S(2)}) %collective-permute-start.4) | collective-permute-done | bytes 352 | tf_op jit(solution)/shard_map/ppermute | solution.py:306
  92.9 1.0 collective-permute-done.5
  94.0 0.1 select_reduce_fusion.1
  94.1 0.6 select_reduce_fusion.2
  94.7 10.2 %collective-permute-done = bf16[320,1792]{1,0:T(8,128)(2,1)} collective-permute-done((bf16[320,1792]{1,0:T(8,128)(2,1)}, bf16[320,1792]{1,0:T(8,128)(2,1)}, u32[]{:S(2)}, u32[]{:S(2)}) %collective-permute-start) | collective-permute-done | bytes 1146912 | tf_op jit(solution)/shard_map/ppermute | solution.py:249
  104.9 9.6 %fusion.2 = bf16[1,1792,2048]{2,1,0:T(8,128)(2,1)} fusion(bf16[320,2048]{1,0:T(8,128)(2,1)S(1)} %bitcast.73, bf16[320,2048]{1,0:T(8,128)(2,1)S(1)} %bitcast.74, bf16[320,1792]{1,0:T(8,128)(2,1)} %collective-permute-done, bf16[320,1792]{1,0:T(8,128)(2,1)} %get-tuple-element.10), kind=kOutput, calls=%fused_computation.3 | convolution fusion | flops 4711120896 | bytes 12255232 | tf_op jit(solution)/shard_map/dot_general | solution.py:312
  (18 shorter events, 0.2 us)
Async XLA Ops:
  2.9 1.0 copy-start
  75.8 13.9 %collective-permute-start.3 = (f32[4,80]{1,0:T(4,128)S(1)}, f32[4,80]{1,0:T(4,128)S(1)}, u32[]{:S(2)}, u32[]{:S(2)}) collective-permute-start(f32[4,80]{1,0:T(4,128)S(1)} %reshape.103), channel_id=1, source_target_pairs={{0,12},{4,0},{8,4},{12,8},{1,13},{5,1},{9,5},{13,9},{2,14},{6,2},{... | collective-permute-start | bytes 3848 | tf_op jit(solution)/shard_map/ppermute | solution.py:301
  76.3 13.4 %collective-permute-start.2 = (f32[4,80]{1,0:T(4,128)S(1)}, f32[4,80]{1,0:T(4,128)S(1)}, u32[]{:S(2)}, u32[]{:S(2)}) collective-permute-start(f32[4,80]{1,0:T(4,128)S(1)} %reshape.103), channel_id=1, source_target_pairs={{0,8},{4,12},{8,0},{12,4},{1,9},{5,13},{9,1},{13,5},{2,10},{6,14},... | collective-permute-start | bytes 3848 | tf_op jit(solution)/shard_map/ppermute | solution.py:301
  76.4 13.4 %collective-permute-start.1 = (f32[4,80]{1,0:T(4,128)S(1)}, f32[4,80]{1,0:T(4,128)S(1)}, u32[]{:S(2)}, u32[]{:S(2)}) collective-permute-start(f32[4,80]{1,0:T(4,128)S(1)} %reshape.103), channel_id=1, source_target_pairs={{0,4},{4,8},{8,12},{12,0},{1,5},{5,9},{9,13},{13,1},{2,6},{6,10},{... | collective-permute-start | bytes 3848 | tf_op jit(solution)/shard_map/ppermute | solution.py:301
  77.9 27.0 %collective-permute-start = (bf16[320,1792]{1,0:T(8,128)(2,1)}, bf16[320,1792]{1,0:T(8,128)(2,1)}, u32[]{:S(2)}, u32[]{:S(2)}) collective-permute-start(bf16[320,1792]{1,0:T(8,128)(2,1)} %get-tuple-element.10), channel_id=1, source_target_pairs={{0,16},{16,0},{1,17},{17,1},{2,18},{18,2},{3,19},{19,3},{4,20},{20... | collective-permute-start | bytes 3440648 | tf_op jit(solution)/shard_map/ppermute | solution.py:249
  88.0 6.1 %copy-start.1 = (s32[128,2]{0,1:T(2,128)S(1)}, s32[128,2]{0,1:T(2,128)}, u32[]{:S(2)}) copy-start(s32[128,2]{0,1:T(2,128)} %param.6) | copy-start | bytes 3076
  89.8 4.1 %collective-permute-start.6 = (f32[1,80]{1,0:T(1,128)S(1)}, f32[1,80]{1,0:T(1,128)S(1)}, u32[]{:S(2)}, u32[]{:S(2)}) collective-permute-start(f32[1,80]{1,0:T(1,128)S(1)} %get-tuple-element.19), channel_id=1, source_target_pairs={{0,3},{1,0},{2,1},{3,2},{4,7},{5,4},{6,5},{7,6},{8,11},{9,8},{10,9... | collective-permute-start | bytes 968 | tf_op jit(solution)/shard_map/ppermute | solution.py:306
  89.8 3.0 %collective-permute-start.4 = (f32[1,80]{1,0:T(1,128)S(1)}, f32[1,80]{1,0:T(1,128)S(1)}, u32[]{:S(2)}, u32[]{:S(2)}) collective-permute-start(f32[1,80]{1,0:T(1,128)S(1)} %get-tuple-element.21), channel_id=1, source_target_pairs={{0,1},{1,2},{2,3},{3,0},{4,5},{5,6},{6,7},{7,4},{8,9},{9,10},{10,1... | collective-permute-start | bytes 968 | tf_op jit(solution)/shard_map/ppermute | solution.py:306
  90.3 3.5 %collective-permute-start.5 = (f32[1,80]{1,0:T(1,128)S(1)}, f32[1,80]{1,0:T(1,128)S(1)}, u32[]{:S(2)}, u32[]{:S(2)}) collective-permute-start(f32[1,80]{1,0:T(1,128)S(1)} %get-tuple-element.20), channel_id=1, source_target_pairs={{0,2},{1,3},{2,0},{3,1},{4,6},{5,7},{6,4},{7,5},{8,10},{9,11},{10,... | collective-permute-start | bytes 968 | tf_op jit(solution)/shard_map/ppermute | solution.py:306

commit v2 on v1

v2 whole, which is shorter than its diff:
```python
import functools
import jax
import jax.numpy as jnp
from jax import lax
from jax.experimental import pallas as pl
from jax.experimental.pallas import tpu as pltpu
from jax.sharding import PartitionSpec as P

MESH = pl.DeviceIdType.MESH


PIECES = 4


def gather_kernel(dims, own_ref, meta_ref, hidden_ref, weight_hbm,
                  back_ref, segw_ref, hid_ref, metas_ref,
                  raw_ref, oth_ref, w_ref, sel_ref, wsel_ref, seg_ref,
                  zs, zr, es, er, xs, xr, ms, mr, hs, hr, ws, loc):
    dp, n, experts, cpd = dims
    d, p, e = lax.axis_index("dp"), lax.axis_index("pipe"), lax.axis_index("expert")
    tokens, cw = own_ref.shape
    slot_count, width = hidden_ref.shape
    capacity = slot_count // experts
    rows = slot_count // PIECES
    tile = 256 if width % 256 == 0 else width
    group = dp * experts
    me = d * experts + e
    has_up, has_down = p < n - 1, p > 0
    masks = []
    m = experts // 2
    while m:
        masks.append(m)
        m //= 2

    def flip(value, mask):
        return value + mask * (1 - 2 * (lax.rem(value // mask, 2)))

    def peer(k):
        t = lax.rem(me + k, group)
        return {"dp": t // experts, "pipe": p, "expert": lax.rem(t, experts)}

    def source(k):
        return lax.rem(me + group - k, group)

    lo, hi = p, n - 1 - p
    both = jnp.where(lo < hi, lo, hi)

    def chunk(a):
        near = jnp.where(lax.rem(a, 2) == 1, p - (a + 1) // 2, p + a // 2)
        far = jnp.where(lo > hi, p - (a - both), p + (a - both))
        return jnp.where(a <= 2 * both, near, far)

    def w_copy(a):
        q = chunk(a)
        return pltpu.make_async_copy(
            weight_hbm.at[:, pl.ds(pl.multiple_of(q * cw, cw), cw)], w_ref.at[q], ws.at[q])

    local = pltpu.make_async_copy(own_ref, raw_ref.at[p, e], loc.at[0])
    local.start()
    local_meta = pltpu.make_async_copy(meta_ref, metas_ref.at[me], loc.at[1])
    local_meta.start()
    local_hidden = pltpu.make_async_copy(hidden_ref, hid_ref.at[0], loc.at[2])
    local_hidden.start()

    barrier = pltpu.get_barrier_semaphore()

    def greet(k, c):
        pl.semaphore_signal(barrier, inc=1, device_id=peer(k), device_id_type=MESH)
        return c

    lax.fori_loop(1, group, greet, 0)

    @pl.when(has_up)
    def _():
        pl.semaphore_signal(barrier, inc=1, device_id={"dp": d, "pipe": p + 1, "expert": e}, device_id_type=MESH)

    @pl.when(has_down)
    def _():
        pl.semaphore_signal(barrier, inc=1, device_id={"dp": d, "pipe": p - 1, "expert": e}, device_id_type=MESH)

    pl.semaphore_wait(barrier, group - 1 + has_up.astype(jnp.int32) + has_down.astype(jnp.int32))

    def meta_copy(k, slot):
        return pltpu.make_async_remote_copy(
            src_ref=meta_ref, dst_ref=metas_ref.at[slot], send_sem=ms.at[k], recv_sem=mr.at[k],
            device_id=peer(k), device_id_type=MESH)

    def z_copy(src, q, s, where):
        return pltpu.make_async_remote_copy(
            src_ref=src, dst_ref=raw_ref.at[q, e], send_sem=zs.at[where, s], recv_sem=zr.at[where, s],
            device_id={"dp": d, "pipe": p + 1 - 2 * where, "expert": e}, device_id_type=MESH)

    def e_copy(ref, i, u, phase, step, src=None):
        block = e
        for j in range(phase):
            if (step // (1 << j)) % 2:
                block = flip(block, masks[j])
        k = (1 << phase) - 1 + step
        view = ref.at[i, block]
        return pltpu.make_async_remote_copy(
            src_ref=view if src is None else src, dst_ref=view, send_sem=es.at[u, k], recv_sem=er.at[u, k],
            device_id={"dp": d, "pipe": p, "expert": flip(e, masks[phase])}, device_id_type=MESH)

    def first(ref, i, u, src=None):
        for phase in range(len(masks)):
            e_copy(ref, i, u, phase, 0, src).start()

    def rest(ref, i, u):
        for phase in range(len(masks)):
            for step in range(1 << phase):
                e_copy(ref, i, u, phase, step).wait_recv()
                arrived = step + (1 << phase)
                for later in range(phase + 1, len(masks)):
                    e_copy(ref, i, u, later, arrived).start()

    def drain(ref, i, u):
        for phase in range(len(masks)):
            for step in range(1 << phase):
                e_copy(ref, i, u, phase, step).wait_send()

    def x_copy(k, i, src):
        return pltpu.make_async_remote_copy(
            src_ref=src, dst_ref=oth_ref.at[(k - 1) * cpd + i, e], send_sem=xs.at[k - 1, i],
            recv_sem=xr.at[k - 1, i],
            device_id={"dp": lax.rem(d + k, dp), "pipe": p, "expert": e}, device_id_type=MESH)

    def x_send(q, src):
        for k in range(1, dp):
            o = lax.rem(d + k, dp)

            @pl.when(q // cpd == o)
            def _():
                x_copy(k, q - o * cpd, src).start()

    def h_copy(k, r):
        span = pl.ds(pl.multiple_of(r * rows, 16), rows)
        return pltpu.make_async_remote_copy(
            src_ref=hidden_ref.at[span, :], dst_ref=hid_ref.at[k, span, :],
            send_sem=hs.at[k - 1, r], recv_sem=hr.at[k - 1, r],
            device_id={"dp": lax.rem(d + k, dp), "pipe": p, "expert": e}, device_id_type=MESH)

    def h_send(r):
        for k in range(1, dp):
            h_copy(k, r).start()

    def metas(k, c):
        meta_copy(k, me).start()
        return c

    lax.fori_loop(1, group, metas, 0)

    @pl.when(has_up)
    def _():
        z_copy(own_ref, p, 0, 0).start()

    @pl.when(has_down)
    def _():
        z_copy(own_ref, p, 0, 1).start()

    first(raw_ref, p, p, own_ref)
    x_send(p, own_ref)
    h_send(0)

    def w_start(a, c):
        w_copy(a).start()
        return c

    lax.fori_loop(0, n, w_start, 0)
    back_ref[...] = jnp.zeros_like(back_ref)

    def metas_done(k, c):
        meta_copy(k, me).wait_send()
        meta_copy(k, source(k)).wait_recv()
        return c

    local_meta.wait()
    lax.fori_loop(1, group, metas_done, 0)
    local.wait()

    slot = lax.broadcasted_iota(jnp.int32, (slot_count, tokens), 0).astype(jnp.float32)

    def build(k, c):
        at = lax.rem(d - k + dp, dp)
        for b in range(experts):
            where = metas_ref[at * experts + b, pl.ds(e, 1), :]
            weight = metas_ref[at * experts + b, pl.ds(experts + e, 1), :]
            chosen = jnp.where(where >= 0.0, where + float(b * capacity), -1.0) == slot
            wsel_ref[k, :, b * tokens:(b + 1) * tokens] = jnp.where(chosen, weight, 0.0).astype(jnp.bfloat16)

            @pl.when(k == 0)
            def _():
                sel_ref[:, b * tokens:(b + 1) * tokens] = jnp.where(chosen, 1.0, 0.0).astype(jnp.bfloat16)
        return c

    lax.fori_loop(0, dp, build, 0)

    def weigh(k, i, data):
        out = jnp.dot(wsel_ref[k], data, preferred_element_type=jnp.float32)
        segw_ref[k, :, pl.ds(pl.multiple_of(i * cw, cw), cw)] = out.astype(jnp.bfloat16)

    def compute(a):
        q = chunk(a)
        rest(raw_ref, q, q)
        data = raw_ref[q].reshape(experts * tokens, cw)
        seg_ref[...] = jnp.dot(sel_ref[...], data, preferred_element_type=jnp.float32).astype(jnp.bfloat16)

        @pl.when(q // cpd == d)
        def _():
            weigh(0, q - d * cpd, data)

        w_copy(a).wait()

        def part(t, c):
            at = pl.multiple_of(t * tile, tile)
            back_ref[:, pl.ds(at, tile)] += lax.dot_general(
                seg_ref[...], w_ref[q, pl.ds(at, tile), :], (((1,), (1,)), ((), ())),
                preferred_element_type=jnp.float32)
            return c

        lax.fori_loop(0, width // tile, part, 0)

    def advance(a, c):
        q = chunk(a)
        below = q < p
        where = jnp.where(below, 0, 1)
        s = jnp.where(below, p - q, q - p)
        z_copy(raw_ref.at[q, e], q, s - 1, where).wait_recv()

        @pl.when((below & has_up) | ((q > p) & has_down))
        def _():
            z_copy(raw_ref.at[q, e], q, s, where).start()

        first(raw_ref, q, q)
        x_send(q, raw_ref.at[q, e])

        @pl.when(a < PIECES)
        def _():
            h_send(a)

        compute(a - 1)
        return c

    lax.fori_loop(1, n, advance, 0)
    reverse = p > d * cpd
    others = (dp - 1) * cpd

    def turn(u):
        i = lax.rem(u, cpd)
        return u // cpd, jnp.where(reverse, cpd - 1 - i, i)

    def x_arrive(u, c):
        kind, i = turn(u)
        x_copy(kind + 1, i, oth_ref.at[kind * cpd + i, e]).wait_recv()
        first(oth_ref, kind * cpd + i, n + kind * cpd + i)
        return c

    compute(n - 1)
    lax.fori_loop(0, others, x_arrive, 0)

    def x_finish(u, c):
        kind, i = turn(u)
        rest(oth_ref, kind * cpd + i, n + kind * cpd + i)
        weigh(kind + 1, i, oth_ref[kind * cpd + i].reshape(experts * tokens, cw))
        return c

    lax.fori_loop(0, others, x_finish, 0)

    def own_drain(q, c):
        drain(raw_ref, q, q)
        return c

    lax.fori_loop(0, n, own_drain, 0)

    def oth_drain(u, c):
        kind, i = u // cpd, lax.rem(u, cpd)
        drain(oth_ref, u, n + u)
        x_copy(kind + 1, i, own_ref).wait_send()
        return c

    lax.fori_loop(0, others, oth_drain, 0)

    def z_drain(s, c):
        @pl.when((p - s >= 0) & has_up)
        def _():
            z_copy(own_ref, p - s, s, 0).wait_send()

        @pl.when((p + s < n) & has_down)
        def _():
            z_copy(own_ref, p + s, s, 1).wait_send()

        return c

    lax.fori_loop(0, n, z_drain, 0)
    for k in range(1, dp):
        for r in range(PIECES):
            h_copy(k, r).wait()
    local_hidden.wait()


def gather(own, meta, hidden, weight, dp, n, experts):
    tokens, cw = own.shape
    slot_count, width = hidden.shape
    cpd = n // dp
    group = dp * experts
    vm = pl.BlockSpec(memory_space=pltpu.VMEM)
    units = n + (dp - 1) * cpd
    dma = pltpu.SemaphoreType.DMA
    return pl.pallas_call(
        functools.partial(gather_kernel, (dp, n, experts, cpd)),
        out_shape=(
            jax.ShapeDtypeStruct((slot_count, width), jnp.float32),
            jax.ShapeDtypeStruct((dp, slot_count, cpd * cw), own.dtype),
            jax.ShapeDtypeStruct((dp, slot_count, width), hidden.dtype),
            jax.ShapeDtypeStruct((group,) + meta.shape, meta.dtype),
        ),
        in_specs=[vm, vm, vm, pl.BlockSpec(memory_space=pl.ANY)],
        out_specs=(vm, vm, vm, vm),
        scratch_shapes=[
            pltpu.VMEM((n, experts, tokens, cw), own.dtype),
            pltpu.VMEM(((dp - 1) * cpd, experts, tokens, cw), own.dtype),
            pltpu.VMEM((n, width, cw), weight.dtype),
            pltpu.VMEM((slot_count, experts * tokens), jnp.bfloat16),
            pltpu.VMEM((dp, slot_count, experts * tokens), jnp.bfloat16),
            pltpu.VMEM((slot_count, cw), jnp.bfloat16),
            dma((2, n)), dma((2, n)),
            dma((units, experts - 1)), dma((units, experts - 1)),
            dma((dp - 1, cpd)), dma((dp - 1, cpd)),
            dma((group,)), dma((group,)),
            dma((dp - 1, PIECES)), dma((dp - 1, PIECES)),
            dma((n,)), dma((3,)),
        ],
        compiler_params=pltpu.CompilerParams(
            collective_id=0, has_side_effects=True, vmem_limit_bytes=56 * 1024 * 1024),
    )(own, meta, hidden, weight)


def body(out_grad, expert_ids, combine_weights, down_weight, saved_pre):
    experts, dp, n = lax.axis_size("expert"), lax.axis_size("dp"), lax.axis_size("pipe")
    e, d = lax.axis_index("expert"), lax.axis_index("dp")
    slot_count = saved_pre.shape[2]
    capacity = slot_count // experts
    tokens = out_grad.shape[0]

    gate_pre = saved_pre[0, 0].astype(jnp.float32)
    up_pre = saved_pre[0, 1].astype(jnp.float32)
    sigmoid_gate = jax.nn.sigmoid(gate_pre)
    activated = gate_pre * sigmoid_gate
    hidden_b = (activated * up_pre).astype(jnp.bfloat16)

    labels = jnp.arange(experts, dtype=jnp.int32)
    hit = expert_ids.T[None, :, :] == labels[:, None, None]
    named = jnp.any(hit, axis=1)
    earlier = jnp.arange(tokens)[:, None] < jnp.arange(tokens)[None, :]
    position = jnp.dot(named.astype(jnp.bfloat16), earlier.astype(jnp.bfloat16),
                       preferred_element_type=jnp.float32)
    position = jnp.where(named, position, -1.0)
    rounded = lax.optimization_barrier(combine_weights.astype(jnp.bfloat16)).astype(jnp.float32)
    weight = jnp.sum(jnp.where(hit, rounded.T[None], 0.0), axis=1)
    meta = jnp.concatenate([position, weight], axis=0)

    back_grad, segw, hidden_all, metas = gather(
        out_grad, meta, hidden_b, down_weight[0], dp, n, experts)

    metas = metas.reshape(dp, experts, 2 * experts, tokens)
    own_metas = lax.dynamic_index_in_dim(metas, d, 0, keepdims=False)
    where = lax.dynamic_index_in_dim(own_metas, e, 1, keepdims=False)
    wt = lax.dynamic_index_in_dim(own_metas, experts + e, 1, keepdims=False)
    slots = jnp.arange(capacity, dtype=jnp.float32)
    chosen = where[:, None, :] == slots[None, :, None]
    weight_row = jnp.sum(jnp.where(chosen, wt[:, None, :], 0.0), axis=2).reshape(slot_count)

    scores = jnp.sum(hidden_b.astype(jnp.float32) * back_grad, axis=1)
    hidden_grad = weight_row[:, None] * back_grad
    gate_grad = hidden_grad * up_pre * sigmoid_gate * (1.0 + gate_pre * (1.0 - sigmoid_gate))
    up_grad = hidden_grad * activated
    pre_grad = jnp.stack([gate_grad, up_grad]).astype(jnp.bfloat16)[None]

    total = scores.reshape(experts, capacity)
    part = total
    for k in range(1, n):
        total = total + lax.ppermute(part, "pipe", [(i, (i + k) % n) for i in range(n)])
    returned = lax.dynamic_update_slice_in_dim(
        jnp.zeros_like(total), lax.dynamic_slice_in_dim(total, e, 1, 0), e, 0)
    for k in range(1, experts):
        block = lax.dynamic_slice_in_dim(total, lax.rem(e + k, experts), 1, 0)
        got = lax.ppermute(block, "expert", [(i, (i + k) % experts) for i in range(experts)])
        returned = lax.dynamic_update_slice_in_dim(returned, got, lax.rem(e - k + experts, experts), 0)
    place = position[:, :, None] == slots[None, None, :]
    by_expert = jnp.sum(jnp.where(place, returned[:, None, :], 0.0), axis=2)
    prob_grad = jnp.sum(jnp.where(hit, by_expert[:, None, :], 0.0), axis=0).T

    w_grad = lax.dot_general(
        hidden_all.reshape(dp * slot_count, -1), segw.reshape(dp * slot_count, -1),
        (((0,), (0,)), ((), ())), preferred_element_type=jnp.float32).astype(jnp.bfloat16)
    return (pre_grad, w_grad[None], prob_grad)


def solution(mesh):
    in_specs = (
        P(("dp", "expert"), "pipe"),
        P(("dp", "expert"), None),
        P(("dp", "expert"), None),
        P("expert", "pipe", None),
        P("expert", None, "dp", "pipe"),
    )
    out_specs = (
        P("expert", None, "dp", "pipe"),
        P("expert", "pipe", "dp"),
        P(("dp", "expert"), None),
    )
    return jax.shard_map(body, mesh=mesh, in_specs=in_specs, out_specs=out_specs, check_vma=False)
```

time: 115 us -> 97.1 us (0.84)
  matrix products: 30.3 us -> 9.75 us
  Pallas kernels: 50.1 us -> 63.7 us
  waiting for transfers between devices: 13.1 us -> 2.79 us
  local copies, waits for them, and re-layouts: 10.7 us -> 1.14 us
  other arithmetic: 5.79 us -> 14.6 us
    dot_general x5 -> x1, matrix products: 30.1 us -> 9.62 us  [body(): lax.dot_general(hidden_all.reshape(dp * slot_count, -1), segw.reshape(dp...]
    pallas_call x1, Pallas kernels: 50.1 us -> 63.7 us  [gather(): pl.pallas_call(functools.partial(gather_kernel, (dp, n, experts, cpd)), o...]
    ppermute x1 -> x0, waiting for transfers between devices: 10.2 us -> none  [body(): lax.ppermute(hidden_b, 'dp', [(i, (i + k) % dp) for i in range(dp)])]
    convert_element_type x3 -> x0, local copies, waits for them, and re-layouts: 6.04 us -> none  [route(): return out.astype(jnp.bfloat16).reshape(slot_count, -1)]
    another operation x1 -> x2, other arithmetic: 2.85 us -> 7.77 us  [body(): pre_grad = jnp.stack([gate_grad, up_grad]).astype(jnp.bfloat16)[None]]
    unnamed x7 -> x6, local copies, waits for them, and re-layouts: 4.29 us -> 0.01 us
    convert_element_type x0 -> x1, other arithmetic: none -> 3.31 us  [body(): hidden_b = (activated * up_pre).astype(jnp.bfloat16)]
  transfers between devices with their start and end apart: 7 -> 6, of which waited for: 3 -> 2; matrix products, arithmetic and copies ran while one was open for 11% -> 13% of each run, Pallas kernels for 0% -> 0%
where the time goes in v2:
time: 97.1 us; the launch traced here: 96.8 us
  Pallas kernels  63.7 us (66%)
  other arithmetic  14.6 us (15%)
  matrix products  9.75 us (10%)
  starting transfers between devices  4.04 us (4%)
  waiting for transfers between devices  2.79 us (3%)
  local copies, waits for them, and re-layouts  1.14 us (1%)
    pallas_call x1, Pallas kernels, gather(): pl.pallas_call(functools.partial(gather_kernel, (dp, n, experts, cpd)), o...  63.7 us
    dot_general x1, matrix products, body(): lax.dot_general(hidden_all.reshape(dp * slot_count, -1), segw.reshape(dp...  9.62 us
    another operation x2, other arithmetic, body(): pre_grad = jnp.stack([gate_grad, up_grad]).astype(jnp.bfloat16)[None]  7.77 us
    convert_element_type x1, other arithmetic, body(): hidden_b = (activated * up_pre).astype(jnp.bfloat16)  3.31 us
    ppermute x3, waiting for transfers between devices, body(): lax.ppermute(block, 'expert', [(i, (i + k) % experts) for i in range(expe...  2.78 us
    ppermute x3, starting transfers between devices, body(): lax.ppermute(part, 'pipe', [(i, (i + k) % n) for i in range(n)])  2.24 us
  transfers between devices with their start and end apart: 6, of which 2 were waited for; matrix products, arithmetic and copies ran while one was open for 13% of the time, Pallas kernels for 0%

profile of v2, /device:TPU:0, one launch (start us, length us, event | category | flops | bytes accessed | tf_op | source)
XLA Modules:
  0.0 96.8 jit_solution(16161780897274172490)
XLA Ops:
  0.6 0.7 fusion.11
  1.3 0.7 convert_element_type.35
  2.0 0.7 select_reduce_fusion.3
  2.7 0.1 convolution_select_fusion
  2.8 3.3 %fusion.1.hidden_ref = bf16[320,1792]{1,0:T(8,128)(2,1)} fusion(bf16[1,2,320,1792]{3,2,1,0:T(8,128)(2,1)} %param.9), kind=kLoop, calls=%fused_computation.7 | loop fusion | flops 4587520 | bytes 3440640 | tf_op jit(solution)/shard_map/convert_element_type | solution.py:348
  6.2 0.6 pad_maximum_fusion.1.meta_ref
  6.8 0.0 copy-start
  6.8 63.7 %shard_map.76 = (f32[320,1792]{1,0:T(8,128)}, bf16[2,320,2048]{2,1,0:T(8,128)(2,1)}, bf16[2,320,1792]{2,1,0:T(8,128)(2,1)}, f32[8,8,128]{2,1,0:T(8,128)}) custom-call(bf16[128,1024]{1,0:T(8,128)(2,1)} %own_ref.1, f32[8,128]{1,0:T(8,128)} %pad_maximum_fusion.1.meta_ref, bf16[320,1792]{1,0:T(8,128)(2,1)} %fusion.1.hidden_ref, bf16[1792,4096]{1,0:T(8,128)(2,1)} %bitcast.41), custom_call_target="tpu_custom_call" | custom-call | tf_op jit(solution)/shard_map/pallas_call | solution.py:308
  70.5 0.8 constant_dynamic-slice_fusion.5
  71.3 0.1 select_reduce_fusion.1
  71.5 0.1 mul.36
  71.5 0.0 copy-done
  71.5 4.8 %fusion.10 = (bf16[1,1,320,1792]{3,2,1,0:T(8,128)(2,1)S(1)}, bf16[1,1,320,1792]{3,2,1,0:T(8,128)(2,1)}, f32[320]{0:T(512)S(1)}) fusion(f32[320,1792]{1,0:T(8,128)} %get-tuple-element.8, f32[320]{0:T(512)S(1)} %mul.36, bf16[1,2,320,1792]{3,2,1,0:T(8,128)(2,1)S(1)} %copy-done), kind=kLoop, calls=%fused_computation.19 | loop fusion | flops 12041920 | bytes 6883840 | tf_op jit(solution)/shard_map/stack | solution.py:376
  76.3 0.1 reshape.81
  76.4 1.6 %collective-permute-start.2 = (f32[4,80]{1,0:T(4,128)S(1)}, f32[4,80]{1,0:T(4,128)S(1)}, u32[]{:S(2)}, u32[]{:S(2)}) collective-permute-start(f32[4,80]{1,0:T(4,128)S(1)} %reshape.81), channel_id=1, source_target_pairs={{0,12},{4,0},{8,4},{12,8},{1,13},{5,1},{9,5},{13,9},{2,14},{6,2},{... | collective-permute-start | bytes 3848 | tf_op jit(solution)/shard_map/ppermute | solution.py:381
  78.0 0.0 collective-permute-start.1
  78.0 0.6 collective-permute-start
  78.6 3.0 %pad_maximum_fusion = bf16[1,2,320,1792]{3,2,1,0:T(8,128)(2,1)} fusion(bf16[1,1,320,1792]{3,2,1,0:T(8,128)(2,1)} %get-tuple-element.12, bf16[1,1,320,1792]{3,2,1,0:T(8,128)(2,1)S(1)} %get-tuple-element.11), kind=kLoop, calls=%fused_computation.15 | loop fusion | flops 1146880 | bytes 4587520 | tf_op jit(solution)/shard_map/stack | solution.py:376
  81.6 0.0 copy-done.2
  81.6 9.6 %fusion = bf16[1,1792,2048]{2,1,0:T(8,128)(2,1)} fusion(bf16[2,320,1792]{2,1,0:T(8,128)(2,1)} %get-tuple-element.9, bf16[2,320,2048]{2,1,0:T(8,128)(2,1)S(1)} %copy-done.2), kind=kOutput, calls=%fused_computation.1 | convolution fusion | flops 4701290496 | bytes 12255232 | tf_op jit(solution)/shard_map/dot_general | solution.py:392
  91.3 0.0 collective-permute-done.2
  91.3 0.0 collective-permute-done.1
  91.3 0.0 collective-permute-done
  91.3 1.1 %collective-permute-start.5 = (f32[1,80]{1,0:T(1,128)S(1)}, f32[1,80]{1,0:T(1,128)S(1)}, u32[]{:S(2)}, u32[]{:S(2)}) collective-permute-start(f32[1,80]{1,0:T(1,128)S(1)} %get-tuple-element.16), channel_id=1, source_target_pairs={{0,3},{1,0},{2,1},{3,2},{4,7},{5,4},{6,5},{7,6},{8,11},{9,8},{10,9... | collective-permute-start | bytes 968 | tf_op jit(solution)/shard_map/ppermute | solution.py:386
  92.4 0.0 collective-permute-start.3
  92.4 0.7 collective-permute-start.4
  93.2 2.2 %collective-permute-done.3 = f32[1,80]{1,0:T(1,128)S(1)} collective-permute-done((f32[1,80]{1,0:T(1,128)S(1)}, f32[1,80]{1,0:T(1,128)S(1)}, u32[]{:S(2)}, u32[]{:S(2)}) %collective-permute-start.3) | collective-permute-done | bytes 352 | tf_op jit(solution)/shard_map/ppermute | solution.py:386
  95.4 0.6 collective-permute-done.4
  96.0 0.0 collective-permute-done.5
  96.0 0.1 select_reduce_fusion
  96.2 0.0 copy-done.1
  96.2 0.6 select_reduce_fusion.2
  (10 shorter events, 0.2 us)
Async XLA Ops:
  6.8 64.8 %copy-start = (bf16[1,2,320,1792]{3,2,1,0:T(8,128)(2,1)S(1)}, bf16[1,2,320,1792]{3,2,1,0:T(8,128)(2,1)}, u32[]{:S(2)}) copy-start(bf16[1,2,320,1792]{3,2,1,0:T(8,128)(2,1)} %param.9) | copy-start | bytes 6881284
  76.4 14.9 %collective-permute-start.2 = (f32[4,80]{1,0:T(4,128)S(1)}, f32[4,80]{1,0:T(4,128)S(1)}, u32[]{:S(2)}, u32[]{:S(2)}) collective-permute-start(f32[4,80]{1,0:T(4,128)S(1)} %reshape.81), channel_id=1, source_target_pairs={{0,12},{4,0},{8,4},{12,8},{1,13},{5,1},{9,5},{13,9},{2,14},{6,2},{... | collective-permute-start | bytes 3848 | tf_op jit(solution)/shard_map/ppermute | solution.py:381
  78.0 13.3 %collective-permute-start.1 = (f32[4,80]{1,0:T(4,128)S(1)}, f32[4,80]{1,0:T(4,128)S(1)}, u32[]{:S(2)}, u32[]{:S(2)}) collective-permute-start(f32[4,80]{1,0:T(4,128)S(1)} %reshape.81), channel_id=1, source_target_pairs={{0,8},{4,12},{8,0},{12,4},{1,9},{5,13},{9,1},{13,5},{2,10},{6,14},... | collective-permute-start | bytes 3848 | tf_op jit(solution)/shard_map/ppermute | solution.py:381
  78.0 13.3 %collective-permute-start = (f32[4,80]{1,0:T(4,128)S(1)}, f32[4,80]{1,0:T(4,128)S(1)}, u32[]{:S(2)}, u32[]{:S(2)}) collective-permute-start(f32[4,80]{1,0:T(4,128)S(1)} %reshape.81), channel_id=1, source_target_pairs={{0,4},{4,8},{8,12},{12,0},{1,5},{5,9},{9,13},{13,1},{2,6},{6,10},{... | collective-permute-start | bytes 3848 | tf_op jit(solution)/shard_map/ppermute | solution.py:381
  78.6 3.0 %copy-start.2 = (bf16[2,320,2048]{2,1,0:T(8,128)(2,1)S(1)}, bf16[2,320,2048]{2,1,0:T(8,128)(2,1)}, u32[]{:S(2)}) copy-start(bf16[2,320,2048]{2,1,0:T(8,128)(2,1)} %get-tuple-element.10) | copy-start | bytes 7864324
  81.6 14.5 %copy-start.1 = (s32[128,2]{0,1:T(2,128)S(1)}, s32[128,2]{0,1:T(2,128)}, u32[]{:S(2)}) copy-start(s32[128,2]{0,1:T(2,128)} %param.6) | copy-start | bytes 3076
  91.3 4.7 %collective-permute-start.5 = (f32[1,80]{1,0:T(1,128)S(1)}, f32[1,80]{1,0:T(1,128)S(1)}, u32[]{:S(2)}, u32[]{:S(2)}) collective-permute-start(f32[1,80]{1,0:T(1,128)S(1)} %get-tuple-element.16), channel_id=1, source_target_pairs={{0,3},{1,0},{2,1},{3,2},{4,7},{5,4},{6,5},{7,6},{8,11},{9,8},{10,9... | collective-permute-start | bytes 968 | tf_op jit(solution)/shard_map/ppermute | solution.py:386
  92.4 3.0 %collective-permute-start.3 = (f32[1,80]{1,0:T(1,128)S(1)}, f32[1,80]{1,0:T(1,128)S(1)}, u32[]{:S(2)}, u32[]{:S(2)}) collective-permute-start(f32[1,80]{1,0:T(1,128)S(1)} %get-tuple-element.18), channel_id=1, source_target_pairs={{0,1},{1,2},{2,3},{3,0},{4,5},{5,6},{6,7},{7,4},{8,9},{9,10},{10,1... | collective-permute-start | bytes 968 | tf_op jit(solution)/shard_map/ppermute | solution.py:386
  92.4 3.6 %collective-permute-start.4 = (f32[1,80]{1,0:T(1,128)S(1)}, f32[1,80]{1,0:T(1,128)S(1)}, u32[]{:S(2)}, u32[]{:S(2)}) collective-permute-start(f32[1,80]{1,0:T(1,128)S(1)} %get-tuple-element.17), channel_id=1, source_target_pairs={{0,2},{1,3},{2,0},{3,1},{4,6},{5,7},{6,4},{7,5},{8,10},{9,11},{10,... | collective-permute-start | bytes 968 | tf_op jit(solution)/shard_map/ppermute | solution.py:386

commit v3 on v2

--- a/solution.py
+++ b/solution.py
@@ -12,14 +12,14 @@
 PIECES = 4
 
 
-def gather_kernel(dims, own_ref, meta_ref, hidden_ref, weight_hbm,
-                  back_ref, segw_ref, hid_ref, metas_ref,
-                  raw_ref, oth_ref, w_ref, sel_ref, wsel_ref, seg_ref,
-                  zs, zr, es, er, xs, xr, ms, mr, hs, hr, ws, loc):
+def gather_kernel(dims, own_ref, meta_ref, saved_hbm, weight_hbm,
+                  pre_ref, segw_ref, hid_ref, score_ref,
+                  raw_ref, oth_ref, w_ref, sel_ref, wsel_ref, seg_ref, back_ref, saved_ref, column_ref, metas_ref,
+                  zs, zr, es, er, xs, xr, ms, mr, hs, hr, ss, sr, ws, loc):
     dp, n, experts, cpd = dims
     d, p, e = lax.axis_index("dp"), lax.axis_index("pipe"), lax.axis_index("expert")
     tokens, cw = own_ref.shape
-    slot_count, width = hidden_ref.shape
+    slot_count, width = back_ref.shape
     capacity = slot_count // experts
     rows = slot_count // PIECES
     tile = 256 if width % 256 == 0 else width
@@ -59,8 +59,8 @@
     local.start()
     local_meta = pltpu.make_async_copy(meta_ref, metas_ref.at[me], loc.at[1])
     local_meta.start()
-    local_hidden = pltpu.make_async_copy(hidden_ref, hid_ref.at[0], loc.at[2])
-    local_hidden.start()
+    local_saved = pltpu.make_async_copy(saved_hbm, saved_ref, loc.at[2])
+    local_saved.start()
 
     barrier = pltpu.get_barrier_semaphore()
 
@@ -70,15 +70,24 @@
 
     lax.fori_loop(1, group, greet, 0)
 
-    @pl.when(has_up)
-    def _():
-        pl.semaphore_signal(barrier, inc=1, device_id={"dp": d, "pipe": p + 1, "expert": e}, device_id_type=MESH)
-
-    @pl.when(has_down)
-    def _():
-        pl.semaphore_signal(barrier, inc=1, device_id={"dp": d, "pipe": p - 1, "expert": e}, device_id_type=MESH)
-
-    pl.semaphore_wait(barrier, group - 1 + has_up.astype(jnp.int32) + has_down.astype(jnp.int32))
+    team = n * experts
+    mine = p * experts + e
+
+    def mate(k):
+        t = lax.rem(mine + k, team)
+        return {"dp": d, "pipe": t // experts, "expert": lax.rem(t, experts)}
+
+    def greet_mate(k, c):
+        pl.semaphore_signal(barrier, inc=1, device_id=mate(k), device_id_type=MESH)
+        return c
+
+    lax.fori_loop(1, team, greet_mate, 0)
+    pl.semaphore_wait(barrier, group + team - 2)
+
+    def score_copy(k, slot):
+        return pltpu.make_async_remote_copy(
+            src_ref=score_ref.at[mine], dst_ref=score_ref.at[slot], send_sem=ss.at[k], recv_sem=sr.at[k],
+            device_id=mate(k), device_id_type=MESH)
 
     def meta_copy(k, slot):
         return pltpu.make_async_remote_copy(
@@ -135,7 +144,7 @@
     def h_copy(k, r):
         span = pl.ds(pl.multiple_of(r * rows, 16), rows)
         return pltpu.make_async_remote_copy(
-            src_ref=hidden_ref.at[span, :], dst_ref=hid_ref.at[k, span, :],
+            src_ref=hid_ref.at[0, span, :], dst_ref=hid_ref.at[k, span, :],
             send_sem=hs.at[k - 1, r], recv_sem=hr.at[k - 1, r],
             device_id={"dp": lax.rem(d + k, dp), "pipe": p, "expert": e}, device_id_type=MESH)
 
@@ -159,13 +168,28 @@
 
     first(raw_ref, p, p, own_ref)
     x_send(p, own_ref)
-    h_send(0)
 
     def w_start(a, c):
         w_copy(a).start()
         return c
 
     lax.fori_loop(0, n, w_start, 0)
+    local_saved.wait()
+    step_rows = 16
+
+    def pres(t):
+        at = pl.ds(pl.multiple_of(t * step_rows, step_rows), step_rows)
+        gate = saved_ref[0, at, :].astype(jnp.float32)
+        up = saved_ref[1, at, :].astype(jnp.float32)
+        sig = jax.nn.sigmoid(gate)
+        return at, gate, up, sig, gate * sig
+
+    def make_hidden(t, c):
+        at, gate, up, sig, activated = pres(t)
+        hid_ref[0, at, :] = (activated * up).astype(jnp.bfloat16)
+        return c
+
+    lax.fori_loop(0, slot_count // step_rows, make_hidden, 0)
     back_ref[...] = jnp.zeros_like(back_ref)
 
     def metas_done(k, c):
@@ -177,6 +201,7 @@
     lax.fori_loop(1, group, metas_done, 0)
     local.wait()
 
+    h_send(0)
     slot = lax.broadcasted_iota(jnp.int32, (slot_count, tokens), 0).astype(jnp.float32)
 
     def build(k, c):
@@ -219,7 +244,7 @@
 
         lax.fori_loop(0, width // tile, part, 0)
 
-    def advance(a, c):
+    def arrive(a):
         q = chunk(a)
         below = q < p
         where = jnp.where(below, 0, 1)
@@ -233,14 +258,22 @@
         first(raw_ref, q, q)
         x_send(q, raw_ref.at[q, e])
 
-        @pl.when(a < PIECES)
-        def _():
-            h_send(a)
-
-        compute(a - 1)
-        return c
-
-    lax.fori_loop(1, n, advance, 0)
+        @pl.when(a == 1)
+        def _():
+            h_send(1)
+
+        @pl.when(a == n - 1)
+        def _():
+            for r in range(2, PIECES):
+                h_send(r)
+
+    def advance(a, c):
+        arrive(a)
+        compute(a - 2)
+        return c
+
+    arrive(jnp.int32(1))
+    lax.fori_loop(2, n, advance, 0)
     reverse = p > d * cpd
     others = (dp - 1) * cpd
 
@@ -254,8 +287,30 @@
         first(oth_ref, kind * cpd + i, n + kind * cpd + i)
         return c
 
-    compute(n - 1)
-    lax.fori_loop(0, others, x_arrive, 0)
+    x_arrive(0, 0)
+    lax.fori_loop(n - 2, n, lambda a, c: (compute(a), c)[1], 0)
+
+    def finish(t, c):
+        at, gate, up, sig, activated = pres(t)
+        back = back_ref[at, :]
+        score = jnp.sum(hid_ref[0, at, :].astype(jnp.float32) * back, axis=1, keepdims=True)
+        column_ref[at, :] = jnp.broadcast_to(score, (step_rows, 128))
+        weight_row = jnp.sum(wsel_ref[0, at, :].astype(jnp.float32), axis=1, keepdims=True)
+        grad = weight_row * back
+        pre_ref[0, at, :] = (grad * up * sig * (1.0 + gate * (1.0 - sig))).astype(jnp.bfloat16)
+        pre_ref[1, at, :] = (grad * activated).astype(jnp.bfloat16)
+        return c
+
+    column_ref[...] = jnp.zeros_like(column_ref)
+    lax.fori_loop(0, slot_count // step_rows, finish, 0)
+    score_ref[mine] = jnp.transpose(column_ref[...])[0:8, :]
+    lax.fori_loop(1, others, x_arrive, 0)
+
+    def score_send(k, c):
+        score_copy(k, mine).start()
+        return c
+
+    lax.fori_loop(1, team, score_send, 0)
 
     def x_finish(u, c):
         kind, i = turn(u)
@@ -294,12 +349,20 @@
     for k in range(1, dp):
         for r in range(PIECES):
             h_copy(k, r).wait()
-    local_hidden.wait()
-
-
-def gather(own, meta, hidden, weight, dp, n, experts):
+
+    def score_done(k, c):
+        score_copy(k, mine).wait_send()
+        score_copy(k, lax.rem(mine + team - k, team)).wait_recv()
+        return c
+
+    lax.fori_loop(1, team, score_done, 0)
+
+
+def gather(own, meta, saved, weight, dp, n, experts):
     tokens, cw = own.shape
-    slot_count, width = hidden.shape
+    _, slot_count, width = saved.shape
+    padded = -(-slot_count // 128) * 128
+    hbm = pl.BlockSpec(memory_space=pl.ANY)
     cpd = n // dp
     group = dp * experts
     vm = pl.BlockSpec(memory_space=pltpu.VMEM)
@@ -308,12 +371,12 @@
     return pl.pallas_call(
         functools.partial(gather_kernel, (dp, n, experts, cpd)),
         out_shape=(
-            jax.ShapeDtypeStruct((slot_count, width), jnp.float32),
+            jax.ShapeDtypeStruct((2, slot_count, width), saved.dtype),
             jax.ShapeDtypeStruct((dp, slot_count, cpd * cw), own.dtype),
-            jax.ShapeDtypeStruct((dp, slot_count, width), hidden.dtype),
-            jax.ShapeDtypeStruct((group,) + meta.shape, meta.dtype),
+            jax.ShapeDtypeStruct((dp, slot_count, width), jnp.bfloat16),
+            jax.ShapeDtypeStruct((n * experts, 8, padded), jnp.float32),
         ),
-        in_specs=[vm, vm, vm, pl.BlockSpec(memory_space=pl.ANY)],
+        in_specs=[vm, vm, hbm, hbm],
         out_specs=(vm, vm, vm, vm),
         scratch_shapes=[
             pltpu.VMEM((n, experts, tokens, cw), own.dtype),
@@ -322,30 +385,29 @@
             pltpu.VMEM((slot_count, experts * tokens), jnp.bfloat16),
             pltpu.VMEM((dp, slot_count, experts * tokens), jnp.bfloat16),
             pltpu.VMEM((slot_count, cw), jnp.bfloat16),
+            pltpu.VMEM((slot_count, width), jnp.float32),
+            pltpu.VMEM((2, slot_count, width), saved.dtype),
+            pltpu.VMEM((padded, 128), jnp.float32),
+            pltpu.VMEM((group,) + meta.shape, meta.dtype),
             dma((2, n)), dma((2, n)),
             dma((units, experts - 1)), dma((units, experts - 1)),
             dma((dp - 1, cpd)), dma((dp - 1, cpd)),
             dma((group,)), dma((group,)),
             dma((dp - 1, PIECES)), dma((dp - 1, PIECES)),
+            dma((n * experts,)), dma((n * experts,)),
             dma((n,)), dma((3,)),
         ],
         compiler_params=pltpu.CompilerParams(
             collective_id=0, has_side_effects=True, vmem_limit_bytes=56 * 1024 * 1024),
-    )(own, meta, hidden, weight)
+    )(own, meta, saved, weight)
 
 
 def body(out_grad, expert_ids, combine_weights, down_weight, saved_pre):
     experts, dp, n = lax.axis_size("expert"), lax.axis_size("dp"), lax.axis_size("pipe")
-    e, d = lax.axis_index("expert"), lax.axis_index("dp")
+    e = lax.axis_index("expert")
     slot_count = saved_pre.shape[2]
     capacity = slot_count // experts
     tokens = out_grad.shape[0]
-
-    gate_pre = saved_pre[0, 0].astype(jnp.float32)
-    up_pre = saved_pre[0, 1].astype(jnp.float32)
-    sigmoid_gate = jax.nn.sigmoid(gate_pre)
-    activated = gate_pre * sigmoid_gate
-    hidden_b = (activated * up_pre).astype(jnp.bfloat16)
 
     labels = jnp.arange(experts, dtype=jnp.int32)
     hit = expert_ids.T[None, :, :] == labels[:, None, None]
@@ -358,33 +420,11 @@
     weight = jnp.sum(jnp.where(hit, rounded.T[None], 0.0), axis=1)
     meta = jnp.concatenate([position, weight], axis=0)
 
-    back_grad, segw, hidden_all, metas = gather(
-        out_grad, meta, hidden_b, down_weight[0], dp, n, experts)
-
-    metas = metas.reshape(dp, experts, 2 * experts, tokens)
-    own_metas = lax.dynamic_index_in_dim(metas, d, 0, keepdims=False)
-    where = lax.dynamic_index_in_dim(own_metas, e, 1, keepdims=False)
-    wt = lax.dynamic_index_in_dim(own_metas, experts + e, 1, keepdims=False)
+    pre_grad, segw, hidden_all, scores = gather(
+        out_grad, meta, saved_pre[0], down_weight[0], dp, n, experts)
     slots = jnp.arange(capacity, dtype=jnp.float32)
-    chosen = where[:, None, :] == slots[None, :, None]
-    weight_row = jnp.sum(jnp.where(chosen, wt[:, None, :], 0.0), axis=2).reshape(slot_count)
-
-    scores = jnp.sum(hidden_b.astype(jnp.float32) * back_grad, axis=1)
-    hidden_grad = weight_row[:, None] * back_grad
-    gate_grad = hidden_grad * up_pre * sigmoid_gate * (1.0 + gate_pre * (1.0 - sigmoid_gate))
-    up_grad = hidden_grad * activated
-    pre_grad = jnp.stack([gate_grad, up_grad]).astype(jnp.bfloat16)[None]
-
-    total = scores.reshape(experts, capacity)
-    part = total
-    for k in range(1, n):
-        total = total + lax.ppermute(part, "pipe", [(i, (i + k) % n) for i in range(n)])
-    returned = lax.dynamic_update_slice_in_dim(
-        jnp.zeros_like(total), lax.dynamic_slice_in_dim(total, e, 1, 0), e, 0)
-    for k in range(1, experts):
-        block = lax.dynamic_slice_in_dim(total, lax.rem(e + k, experts), 1, 0)
-        got = lax.ppermute(block, "expert", [(i, (i + k) % experts) for i in range(experts)])
-        returned = lax.dynamic_update_slice_in_dim(returned, got, lax.rem(e - k + experts, experts), 0)
+    total = jnp.sum(scores.reshape(n, experts, 8, -1)[:, :, 0, :], axis=0)
+    returned = lax.dynamic_slice_in_dim(total, e * capacity, capacity, 1)
     place = position[:, :, None] == slots[None, None, :]
     by_expert = jnp.sum(jnp.where(place, returned[:, None, :], 0.0), axis=2)
     prob_grad = jnp.sum(jnp.where(hit, by_expert[:, None, :], 0.0), axis=0).T
@@ -392,7 +432,7 @@
     w_grad = lax.dot_general(
         hidden_all.reshape(dp * slot_count, -1), segw.reshape(dp * slot_count, -1),
         (((0,), (0,)), ((), ())), preferred_element_type=jnp.float32).astype(jnp.bfloat16)
-    return (pre_grad, w_grad[None], prob_grad)
+    return (pre_grad[None], w_grad[None], prob_grad)
 
 
 def solution(mesh):

time: 97.1 us -> 75.5 us (0.78)
  other arithmetic: 14.6 us -> 4.34 us
  Pallas kernels: 63.7 us -> 58.5 us
  starting transfers between devices: 4.04 us -> 0 us
  waiting for transfers between devices: 2.79 us -> 0 us
    another operation x2 -> x0, other arithmetic: 7.77 us -> none  [body(): pre_grad = jnp.stack([gate_grad, up_grad]).astype(jnp.bfloat16)[None]]
    pallas_call x1, Pallas kernels: 63.7 us -> 58.5 us  [gather(): pl.pallas_call(functools.partial(gather_kernel, (dp, n, experts, cpd)), o...]
    ppermute x6 -> x0, starting transfers between devices: 4.04 us -> none  [the longest x3 2.24 us: body(): lax.ppermute(part, 'pipe', [(i, (i + k) % n) for i in range(n)])]
    convert_element_type x1 -> x0, other arithmetic: 3.31 us -> none  [body(): hidden_b = (activated * up_pre).astype(jnp.bfloat16)]
    ppermute x6 -> x0, waiting for transfers between devices: 2.79 us -> none  [the longest x3 2.78 us: body(): lax.ppermute(block, 'expert', [(i, (i + k) % experts) for i in range(expe...]
    unnamed x6 -> x5, local copies, waits for them, and re-layouts: 0.01 us -> 1.39 us
  transfers between devices with their start and end apart: 6 -> 0, of which waited for: 2 -> 0; matrix products, arithmetic and copies ran while one was open for 13% -> 0% of each run, Pallas kernels for 0% -> 0%
where the time goes in v3:
time: 75.5 us; the launch traced here: 75.3 us
  Pallas kernels  58.5 us (77%)
  matrix products  10.3 us (14%)
  other arithmetic  4.34 us (6%)
  local copies, waits for them, and re-layouts  1.47 us (2%)
    pallas_call x1, Pallas kernels, gather(): pl.pallas_call(functools.partial(gather_kernel, (dp, n, experts, cpd)), o...  58.5 us
    dot_general x1, matrix products, body(): lax.dot_general(hidden_all.reshape(dp * slot_count, -1), segw.reshape(dp...  10.2 us

profile of v3, /device:TPU:0, one launch (start us, length us, event | category | flops | bytes accessed | tf_op | source)
XLA Modules:
  0.0 75.3 jit_solution(2941566535465435628)
XLA Ops:
  0.6 0.7 fusion.1
  1.3 0.7 convert_element_type.4
  2.0 0.7 select_reduce_fusion.2
  2.7 0.1 convolution_select_fusion
  2.8 0.6 pad_maximum_fusion.meta_ref
  3.4 0.0 copy-start.1
  3.5 58.5 %shard_map.76 = (bf16[2,320,1792]{2,1,0:T(8,128)(2,1)}, bf16[2,320,2048]{2,1,0:T(8,128)(2,1)}, bf16[2,320,1792]{2,1,0:T(8,128)(2,1)}, f32[16,8,384]{2,1,0:T(8,128)}) custom-call(bf16[128,1024]{1,0:T(8,128)(2,1)} %own_ref.1, f32[8,128]{1,0:T(8,128)} %pad_maximum_fusion.meta_ref, bf16[2,320,1792]{2,1,0:T(8,128)(2,1)} %bitcast.18, bf16[1792,4096]{1,0:T(8,128)(2,1)} %bitcast.17), custom_call_target="tpu_custom_call" | custom-call | tf_op jit(solution)/shard_map/pallas_call | solution.py:371
  61.9 1.0 %slice_reduce_fusion = f32[4,384]{1,0:T(4,128)S(1)} fusion(f32[4,4,8,384]{3,2,1,0:T(8,128)} %bitcast.23), kind=kLoop, calls=%fused_computation.6 | loop fusion | flops 4608 | bytes 30720 | tf_op jit(solution)/shard_map/reduce_sum | solution.py:426
  62.9 0.1 constant_dynamic-slice_fusion
  63.0 0.1 select_reduce_fusion
  63.1 0.0 copy-done.1
  63.1 0.6 select_reduce_fusion.1
  63.7 0.0 copy-start
  63.7 10.2 %fusion = bf16[1,1792,2048]{2,1,0:T(8,128)(2,1)} fusion(bf16[2,320,1792]{2,1,0:T(8,128)(2,1)} %get-tuple-element.8, bf16[2,320,2048]{2,1,0:T(8,128)(2,1)} %get-tuple-element.9), kind=kOutput, calls=%fused_computation.1 | convolution fusion | flops 4701290496 | bytes 12255232 | tf_op jit(solution)/shard_map/dot_general | solution.py:432
  73.9 0.0 copy-done
  73.9 1.4 %copy.9 = bf16[1,2,320,1792]{3,2,1,0:T(8,128)(2,1)} copy(bf16[1,2,320,1792]{3,2,1,0:T(8,128)(2,1)S(1)} %bitcast.19) | data formatting | bytes 4587520
  (1 shorter events, 0.0 us)
Async XLA Ops:
  3.4 59.7 %copy-start.1 = (s32[128,2]{0,1:T(2,128)S(1)}, s32[128,2]{0,1:T(2,128)}, u32[]{:S(2)}) copy-start(s32[128,2]{0,1:T(2,128)} %param.6) | copy-start | bytes 3076
  63.7 10.2 %copy-start = (bf16[2,320,1792]{2,1,0:T(8,128)(2,1)S(1)}, bf16[2,320,1792]{2,1,0:T(8,128)(2,1)}, u32[]{:S(2)}) copy-start(bf16[2,320,1792]{2,1,0:T(8,128)(2,1)} %get-tuple-element.7) | copy-start | bytes 6881284

commit v4 on v3

--- a/solution.py
+++ b/solution.py
@@ -94,57 +94,66 @@
             src_ref=meta_ref, dst_ref=metas_ref.at[slot], send_sem=ms.at[k], recv_sem=mr.at[k],
             device_id=peer(k), device_id_type=MESH)
 
-    def z_copy(src, q, s, where):
-        return pltpu.make_async_remote_copy(
-            src_ref=src, dst_ref=raw_ref.at[q, e], send_sem=zs.at[where, s], recv_sem=zr.at[where, s],
+    half = tokens // 2
+
+    def span(f):
+        return pl.ds(f * half, half)
+
+    def z_copy(src, q, s, where, f):
+        return pltpu.make_async_remote_copy(
+            src_ref=src.at[span(f), :], dst_ref=raw_ref.at[q, e, span(f), :], send_sem=zs.at[where, s, f],
+            recv_sem=zr.at[where, s, f],
             device_id={"dp": d, "pipe": p + 1 - 2 * where, "expert": e}, device_id_type=MESH)
 
-    def e_copy(ref, i, u, phase, step, src=None):
+    def e_copy(ref, i, u, phase, step, f, src=None):
         block = e
         for j in range(phase):
             if (step // (1 << j)) % 2:
                 block = flip(block, masks[j])
         k = (1 << phase) - 1 + step
-        view = ref.at[i, block]
-        return pltpu.make_async_remote_copy(
-            src_ref=view if src is None else src, dst_ref=view, send_sem=es.at[u, k], recv_sem=er.at[u, k],
+        view = ref.at[i, block, span(f), :]
+        return pltpu.make_async_remote_copy(
+            src_ref=view if src is None else src.at[span(f), :], dst_ref=view, send_sem=es.at[u, k, f],
+            recv_sem=er.at[u, k, f],
             device_id={"dp": d, "pipe": p, "expert": flip(e, masks[phase])}, device_id_type=MESH)
 
-    def first(ref, i, u, src=None):
+    def first(ref, i, u, f, src=None):
         for phase in range(len(masks)):
-            e_copy(ref, i, u, phase, 0, src).start()
+            e_copy(ref, i, u, phase, 0, f, src).start()
 
     def rest(ref, i, u):
         for phase in range(len(masks)):
             for step in range(1 << phase):
-                e_copy(ref, i, u, phase, step).wait_recv()
                 arrived = step + (1 << phase)
-                for later in range(phase + 1, len(masks)):
-                    e_copy(ref, i, u, later, arrived).start()
+                for f in range(2):
+                    e_copy(ref, i, u, phase, step, f).wait_recv()
+                    for later in range(phase + 1, len(masks)):
+                        e_copy(ref, i, u, later, arrived, f).start()
 
     def drain(ref, i, u):
         for phase in range(len(masks)):
             for step in range(1 << phase):
-                e_copy(ref, i, u, phase, step).wait_send()
-
-    def x_copy(k, i, src):
-        return pltpu.make_async_remote_copy(
-            src_ref=src, dst_ref=oth_ref.at[(k - 1) * cpd + i, e], send_sem=xs.at[k - 1, i],
-            recv_sem=xr.at[k - 1, i],
+                for f in range(2):
+                    e_copy(ref, i, u, phase, step, f).wait_send()
+
+    def x_copy(k, i, src, f):
+        return pltpu.make_async_remote_copy(
+            src_ref=src.at[span(f), :], dst_ref=oth_ref.at[(k - 1) * cpd + i, e, span(f), :],
+            send_sem=xs.at[k - 1, i, f], recv_sem=xr.at[k - 1, i, f],
             device_id={"dp": lax.rem(d + k, dp), "pipe": p, "expert": e}, device_id_type=MESH)
 
-    def x_send(q, src):
+    def x_send(q, src, f):
         for k in range(1, dp):
             o = lax.rem(d + k, dp)
 
             @pl.when(q // cpd == o)
             def _():
-                x_copy(k, q - o * cpd, src).start()
+                x_copy(k, q - o * cpd, src, f).start()
 
     def h_copy(k, r):
-        span = pl.ds(pl.multiple_of(r * rows, 16), rows)
-        return pltpu.make_async_remote_copy(
-            src_ref=hid_ref.at[0, span, :], dst_ref=hid_ref.at[k, span, :],
+        part = pl.ds(pl.multiple_of(r * rows, 16), rows)
+        return pltpu.make_async_remote_copy(
+            src_ref=hid_ref.at[0, part, :], dst_ref=hid_ref.at[k, part, :],
             send_sem=hs.at[k - 1, r], recv_sem=hr.at[k - 1, r],
             device_id={"dp": lax.rem(d + k, dp), "pipe": p, "expert": e}, device_id_type=MESH)
 
@@ -158,16 +167,17 @@
 
     lax.fori_loop(1, group, metas, 0)
 
-    @pl.when(has_up)
-    def _():
-        z_copy(own_ref, p, 0, 0).start()
-
-    @pl.when(has_down)
-    def _():
-        z_copy(own_ref, p, 0, 1).start()
-
-    first(raw_ref, p, p, own_ref)
-    x_send(p, own_ref)
+    for f in range(2):
+        @pl.when(has_up)
+        def _():
+            z_copy(own_ref, p, 0, 0, f).start()
+
+        @pl.when(has_down)
+        def _():
+            z_copy(own_ref, p, 0, 1, f).start()
+
+        first(raw_ref, p, p, f, own_ref)
+        x_send(p, own_ref, f)
 
     def w_start(a, c):
         w_copy(a).start()
@@ -249,14 +259,15 @@
         below = q < p
         where = jnp.where(below, 0, 1)
         s = jnp.where(below, p - q, q - p)
-        z_copy(raw_ref.at[q, e], q, s - 1, where).wait_recv()
-
-        @pl.when((below & has_up) | ((q > p) & has_down))
-        def _():
-            z_copy(raw_ref.at[q, e], q, s, where).start()
-
-        first(raw_ref, q, q)
-        x_send(q, raw_ref.at[q, e])
+        for f in range(2):
+            z_copy(raw_ref.at[q, e], q, s - 1, where, f).wait_recv()
+
+            @pl.when((below & has_up) | ((q > p) & has_down))
+            def _():
+                z_copy(raw_ref.at[q, e], q, s, where, f).start()
+
+            first(raw_ref, q, q, f)
+            x_send(q, raw_ref.at[q, e], f)
 
         @pl.when(a == 1)
         def _():
@@ -283,8 +294,9 @@
 
     def x_arrive(u, c):
         kind, i = turn(u)
-        x_copy(kind + 1, i, oth_ref.at[kind * cpd + i, e]).wait_recv()
-        first(oth_ref, kind * cpd + i, n + kind * cpd + i)
+        for f in range(2):
+            x_copy(kind + 1, i, oth_ref.at[kind * cpd + i, e], f).wait_recv()
+            first(oth_ref, kind * cpd + i, n + kind * cpd + i, f)
         return c
 
     x_arrive(0, 0)
@@ -329,7 +341,8 @@
     def oth_drain(u, c):
         kind, i = u // cpd, lax.rem(u, cpd)
         drain(oth_ref, u, n + u)
-        x_copy(kind + 1, i, own_ref).wait_send()
+        for f in range(2):
+            x_copy(kind + 1, i, own_ref, f).wait_send()
         return c
 
     lax.fori_loop(0, others, oth_drain, 0)
@@ -337,11 +350,13 @@
     def z_drain(s, c):
         @pl.when((p - s >= 0) & has_up)
         def _():
-            z_copy(own_ref, p - s, s, 0).wait_send()
+            for f in range(2):
+                z_copy(own_ref, p - s, s, 0, f).wait_send()
 
         @pl.when((p + s < n) & has_down)
         def _():
-            z_copy(own_ref, p + s, s, 1).wait_send()
+            for f in range(2):
+                z_copy(own_ref, p + s, s, 1, f).wait_send()
 
         return c
 
@@ -389,9 +404,9 @@
             pltpu.VMEM((2, slot_count, width), saved.dtype),
             pltpu.VMEM((padded, 128), jnp.float32),
             pltpu.VMEM((group,) + meta.shape, meta.dtype),
-            dma((2, n)), dma((2, n)),
-            dma((units, experts - 1)), dma((units, experts - 1)),
-            dma((dp - 1, cpd)), dma((dp - 1, cpd)),
+            dma((2, n, 2)), dma((2, n, 2)),
+            dma((units, experts - 1, 2)), dma((units, experts - 1, 2)),
+            dma((dp - 1, cpd, 2)), dma((dp - 1, cpd, 2)),
             dma((group,)), dma((group,)),
             dma((dp - 1, PIECES)), dma((dp - 1, PIECES)),
             dma((n * experts,)), dma((n * experts,)),

time: 75.5 us -> 76.2 us (level)
  no operation moved by 1% of the time
where the time goes in v4:
time: 76.2 us; the launch traced here: 75.7 us
  Pallas kernels  58.9 us (77%)
  matrix products  10.3 us (14%)
  other arithmetic  4.34 us (6%)
  local copies, waits for them, and re-layouts  1.47 us (2%)
    pallas_call x1, Pallas kernels, gather(): pl.pallas_call(functools.partial(gather_kernel, (dp, n, experts, cpd)), o...  58.9 us
    dot_general x1, matrix products, body(): lax.dot_general(hidden_all.reshape(dp * slot_count, -1), segw.reshape(dp...  10.2 us

profile of v4, /device:TPU:0, one launch (start us, length us, event | category | flops | bytes accessed | tf_op | source)
XLA Modules:
  0.0 75.7 jit_solution(17277893937058353264)
XLA Ops:
  0.6 0.7 fusion.1
  1.3 0.7 convert_element_type.4
  2.0 0.7 select_reduce_fusion.2
  2.7 0.1 convolution_select_fusion
  2.8 0.6 pad_maximum_fusion.meta_ref
  3.4 0.0 copy-start.1
  3.5 58.9 %shard_map.76 = (bf16[2,320,1792]{2,1,0:T(8,128)(2,1)}, bf16[2,320,2048]{2,1,0:T(8,128)(2,1)}, bf16[2,320,1792]{2,1,0:T(8,128)(2,1)}, f32[16,8,384]{2,1,0:T(8,128)}) custom-call(bf16[128,1024]{1,0:T(8,128)(2,1)} %own_ref.1, f32[8,128]{1,0:T(8,128)} %pad_maximum_fusion.meta_ref, bf16[2,320,1792]{2,1,0:T(8,128)(2,1)} %bitcast.18, bf16[1792,4096]{1,0:T(8,128)(2,1)} %bitcast.17), custom_call_target="tpu_custom_call" | custom-call | tf_op jit(solution)/shard_map/pallas_call | solution.py:386
  62.4 1.0 %slice_reduce_fusion = f32[4,384]{1,0:T(4,128)S(1)} fusion(f32[4,4,8,384]{3,2,1,0:T(8,128)} %bitcast.23), kind=kLoop, calls=%fused_computation.6 | loop fusion | flops 4608 | bytes 30720 | tf_op jit(solution)/shard_map/reduce_sum | solution.py:441
  63.4 0.1 constant_dynamic-slice_fusion
  63.4 0.1 select_reduce_fusion
  63.6 0.0 copy-done.1
  63.6 0.6 select_reduce_fusion.1
  64.2 0.0 copy-start
  64.2 10.2 %fusion = bf16[1,1792,2048]{2,1,0:T(8,128)(2,1)} fusion(bf16[2,320,1792]{2,1,0:T(8,128)(2,1)} %get-tuple-element.8, bf16[2,320,2048]{2,1,0:T(8,128)(2,1)} %get-tuple-element.9), kind=kOutput, calls=%fused_computation.1 | convolution fusion | flops 4701290496 | bytes 12255232 | tf_op jit(solution)/shard_map/dot_general | solution.py:447
  74.3 0.0 copy-done
  74.3 1.4 %copy.9 = bf16[1,2,320,1792]{3,2,1,0:T(8,128)(2,1)} copy(bf16[1,2,320,1792]{3,2,1,0:T(8,128)(2,1)S(1)} %bitcast.19) | data formatting | bytes 4587520
  (1 shorter events, 0.0 us)
Async XLA Ops:
  3.4 60.1 %copy-start.1 = (s32[128,2]{0,1:T(2,128)S(1)}, s32[128,2]{0,1:T(2,128)}, u32[]{:S(2)}) copy-start(s32[128,2]{0,1:T(2,128)} %param.6) | copy-start | bytes 3076
  64.2 10.2 %copy-start = (bf16[2,320,1792]{2,1,0:T(8,128)(2,1)S(1)}, bf16[2,320,1792]{2,1,0:T(8,128)(2,1)}, u32[]{:S(2)}) copy-start(bf16[2,320,1792]{2,1,0:T(8,128)(2,1)} %get-tuple-element.7) | copy-start | bytes 6881284
